TPU v7x, 32 devices: a whole 2x2x4 slice. The times are simulated.
32 devices in a mesh: row: 8 (over y, x, core), col: 4 (over z).
Axes of the slice: x: 2, y: 2, z: 4, core: 2. Of those that a mesh axis runs over, the one named last changes fastest.
Arguments:
- covariance: float32 [8192, 8192], P('row', 'col'), may hold values from -8 to 8, as said below
- model_noise: float32 [8192], replicated, may hold values from 0.2 to 1
- east_wind: float32 [2, 64, 128], replicated, may hold values from -0.45 to 0.45
- north_wind: float32 [2, 64, 128], replicated, may hold values from -0.45 to 0.45
Outputs:
- forecast: float32 [8192, 8192], P('row', 'col')
Inputs may be any that keep to these rules, and one draw needn't show every extreme that they name: `covariance`: symmetric.
All inputs are finite; a program needn't handle non-finite values.
Results may differ from a plain program's by a relative error of at most 0.00002.
Values sent between devices are 32-bit elements; how exact they have to be, the bound alone decides.
A program may use at most 128 MiB of HBM per device.

v0:
```python
import jax
import jax.numpy as jnp
from jax import lax
from jax.sharding import PartitionSpec as P

NLON = 128
CYCLES = 2


def extended_2(array, sides, width):
    for axis, dim in sides:
        devices, length = (lax.axis_size(axis), array.shape[dim])
        up = [(i, (i + 1) % devices) for i in range(devices - 1)]
        down = [(j, i) for i, j in up]
        last = lax.slice_in_dim(array, length - width, length, axis=dim)
        first = lax.slice_in_dim(array, 0, width, axis=dim)
        before = lax.ppermute(last, axis, up)
        after = lax.ppermute(first, axis, down)
        array = jnp.concatenate([before, array, after], axis=dim)
    return array


def tendency(padded, east_now, faces_now, lat_axis, expand):
    lon_axis = lat_axis + 1
    lines = padded.shape[lat_axis] - 2
    middle = lax.slice_in_dim(padded, 1, lines + 1, axis=lat_axis)
    eastward = jnp.roll(middle, -1, axis=lon_axis)
    courant = expand(east_now)
    flux_east = jnp.maximum(courant, 0.0) * middle + jnp.minimum(courant, 0.0) * eastward
    flux_west = jnp.roll(flux_east, 1, axis=lon_axis)
    below = lax.slice_in_dim(padded, 0, lines + 1, axis=lat_axis)
    above = lax.slice_in_dim(padded, 1, lines + 2, axis=lat_axis)
    northern = expand(faces_now)
    flux_north = jnp.maximum(northern, 0.0) * below + jnp.minimum(northern, 0.0) * above
    south_in = lax.slice_in_dim(flux_north, 0, lines, axis=lat_axis)
    north_out = lax.slice_in_dim(flux_north, 1, lines + 1, axis=lat_axis)
    return flux_west - flux_east + (south_in - north_out)


def rows_form(values):
    return values[:, :, None]


def cols_form(values):
    return values[None, :, :]


def shaped(matrix, lat_axis):
    if lat_axis == 0:
        return matrix.reshape(matrix.shape[0] // NLON, NLON, matrix.shape[1])
    return matrix.reshape(matrix.shape[0], matrix.shape[1] // NLON, NLON)


def flatten(field, lat_axis):
    if lat_axis == 0:
        return field.reshape(field.shape[0] * NLON, field.shape[2])
    return field.reshape(field.shape[0], field.shape[1] * NLON)


def lines_of(wind, first_line, amount):
    padded = jnp.pad(wind, ((2, 2), (0, 0)))
    return lax.dynamic_slice_in_dim(padded, first_line + 2, amount, 0)


def rim_rows(matrix):
    return extended_2(matrix, (("row", 0),), NLON)


def rim_cols(matrix):
    return extended_2(matrix, (("col", 1),), NLON)


def heun_section(matrix, east_now, north_now, first_line, lat_axis, expand, spread):
    field = shaped(matrix, lat_axis)
    lines = field.shape[lat_axis]
    east_here = lines_of(east_now, first_line, lines)
    faces_here = lines_of(north_now, first_line - 1, lines + 1)
    section_one = field + tendency(
        shaped(spread(matrix), lat_axis), east_here, faces_here, lat_axis, expand
    )
    extended = shaped(spread(flatten(section_one, lat_axis)), lat_axis)
    tend_two = tendency(extended, east_here, faces_here, lat_axis, expand)
    return flatten(0.5 * (field + section_one + tend_two), lat_axis)


def on_device(covariance, model_noise, east_wind, north_wind):
    rows_here = covariance.shape[0]
    cols_here = covariance.shape[1]
    row_first = lax.axis_index("row") * (rows_here // NLON)
    col_first = lax.axis_index("col") * (cols_here // NLON)
    row_ids = lax.axis_index("row") * rows_here + jnp.arange(rows_here, dtype=jnp.int32)
    col_ids = lax.axis_index("col") * cols_here + jnp.arange(cols_here, dtype=jnp.int32)
    noise_rows = lax.dynamic_slice_in_dim(
        model_noise, lax.axis_index("row") * rows_here, rows_here, 0
    )
    diagonal = row_ids[:, None] == col_ids[None, :]
    state = covariance
    for cycle_index in range(CYCLES):
        east_now = east_wind[cycle_index]
        north_now = north_wind[cycle_index]
        after_rows = heun_section(state, east_now, north_now, row_first, 0, rows_form, rim_rows)
        state = heun_section(after_rows, east_now, north_now, col_first, 1, cols_form, rim_cols)
        state = state + jnp.where(diagonal, noise_rows[:, None], 0.0)
    return state


def solution(mesh):
    in_specs = (P("row", "col"), P(), P(), P())
    out_specs = P("row", "col")
    return jax.shard_map(
        on_device, mesh=mesh, in_specs=in_specs, out_specs=out_specs, check_vma=False
    )
```

profile of v0, /device:TPU:2, one launch (start us, length us, event | category | flops | bytes accessed | tf_op | source)
XLA Modules:
  0.0 637.0 jit_solution(12730837203272052402)
XLA Ops:
  9.4 8.7 %slice.408 = f32[8,127,2048]{2,1,0:T(8,128)} slice(f32[8,128,2048]{2,1,0:T(8,128)} %bitcast.62), slice={[0:8], [1:128], [0:2048]} | slice | bytes 16646144 | tf_op jit(solution)/shard_map/jit(_roll_static)/slice | solution.py:27
  29.3 11.8 %pad_maximum_fusion = (f32[1152,2048]{1,0:T(8,128)}, f32[1152,2048]{1,0:T(8,128)}) fusion(f32[1024,2048]{1,0:T(8,128)} %param.4, f32[128,2048]{1,0:T(8,128)S(1)} %collective-permute-done, f32[128,2048]{1,0:T(8,128)S(1)} %collective-permute-done.1), kind=kLoop, calls=%fused_computation.2 | loop fusion | flops 4718592 | bytes 29360128 | tf_op jit(solution)/shard_map/concatenate | solution.py:19
  41.1 11.1 %multiply_add_fusion.3 = f32[9,128,2048]{2,1,0:T(8,128)} fusion(f32[9,128,2048]{2,1,0:T(8,128)} %bitcast.112, f32[9,128,2048]{2,1,0:T(8,128)} %bitcast.111, f32[9,128]{1,0:T(8,128)S(1)} %get-tuple-element.48, f32[9,128]{1,0:T(8,128)S(1)} %get-tuple-element.47), kind=kLoop, calls=%fused_computation.17 | loop fusion | flops 7077888 | bytes 28320768 | tf_op jit(solution)/shard_map/add | solution.py:34
  52.2 21.0 %fusion.27 = f32[8,128,2048]{2,1,0:T(8,128)} fusion(f32[8,128,2048]{2,1,0:T(8,128)} %bitcast.64, f32[9,128,2048]{2,1,0:T(8,128)} %multiply_add_fusion.3, f32[8,128,2048]{2,1,0:T(8,128)} %copy-done.6, f32[8,127,2048]{2,1,0:T(8,128)} %bitcast.93, f32[8,1,2048]{2,1,0:T(1,128)S(1)} %slice.410), kind=kLoop, calls=%fused_computation.65 | loop fusion | flops 10485760 | bytes 50331648 | tf_op jit(solution)/shard_map/add | solution.py:78
  92.2 9.9 %collective-permute-done.3 = f32[128,2048]{1,0:T(8,128)} collective-permute-done((f32[128,2048]{1,0:T(8,128)S(1)}, f32[128,2048]{1,0:T(8,128)}, u32[]{:S(2)}, u32[]{:S(2)}) %collective-permute-start.3) | collective-permute-done | bytes 1048608 | tf_op jit(solution)/shard_map/ppermute | solution.py:18
  110.3 11.1 %multiply_add_fusion.2 = f32[9,128,2048]{2,1,0:T(8,128)} fusion(f32[9,128,2048]{2,1,0:T(8,128)} %bitcast.106, f32[9,128,2048]{2,1,0:T(8,128)} %bitcast.105, f32[9,128]{1,0:T(8,128)S(1)} %get-tuple-element.48, f32[9,128]{1,0:T(8,128)S(1)} %get-tuple-element.47), kind=kLoop, calls=%fused_computation.16 | loop fusion | flops 7077888 | bytes 28320768 | tf_op jit(solution)/shard_map/add | solution.py:34
  121.4 22.2 %fusion.25 = f32[8,128,2048]{2,1,0:T(8,128)} fusion(f32[9,128,2048]{2,1,0:T(8,128)} %multiply_add_fusion.2, f32[8,128,2048]{2,1,0:T(8,128)} %copy-done.7, f32[8,127,2048]{2,1,0:T(8,128)} %bitcast.94, f32[8,1,2048]{2,1,0:T(1,128)S(1)} %slice.416, f32[8,128,2048]{2,1,0:T(8,128)} %bitcast.65, f32[8,128,2048]{2,1,0:T(8,128)} %fusion.27), kind=kLoop, calls=%fused_computation.62 | loop fusion | flops 14680064 | bytes 58720256 | tf_op jit(solution)/shard_map/mul | solution.py:83
  143.5 9.3 %copy.16 = f32[1024,2048]{0,1:T(8,128)} copy(f32[1024,2048]{1,0:T(8,128)} %bitcast.101) | data formatting | bytes 16777216 | tf_op jit(solution)/shard_map/reshape | solution.py:56
  160.9 8.7 %copy.30 = f32[128,8,16,128]{3,2,1,0:T(8,128)} copy(f32[128,8,16,128]{3,1,2,0:T(8,128)} %bitcast.102) | data formatting | bytes 16777216
  178.3 9.0 %pad_maximum_fusion.4 = f32[1024,2304]{0,1:T(8,128)} fusion(f32[1024,128]{0,1:T(8,128)S(1)} %collective-permute-done.5, f32[1024,2048]{0,1:T(8,128)} %copy.16, f32[1024,128]{0,1:T(8,128)S(1)} %collective-permute-done.4), kind=kLoop, calls=%fused_computation.6 | loop fusion | flops 4718592 | bytes 18874368 | tf_op jit(solution)/shard_map/concatenate | solution.py:19
  188.3 8.9 %slice.425 = f32[1024,16,127]{0,2,1:T(8,128)} slice(f32[1024,18,128]{0,2,1:T(8,128)} %bitcast.72), slice={[0:1024], [1:17], [1:128]} | slice | bytes 16646144 | tf_op jit(solution)/shard_map/jit(_roll_static)/slice | solution.py:27
  207.4 21.3 %fusion.21 = f32[1024,16,128]{0,2,1:T(8,128)} fusion(f32[1024,16,128]{0,2,1:T(8,128)} %copy.20, f32[1024,17,128]{0,2,1:T(8,128)} %fusion.3, f32[1024,16,128]{0,2,1:T(8,128)} %copy-done.10, f32[1024,16,127]{0,2,1:T(8,128)} %bitcast.97, f32[1024,16,1]{0,2,1:T(1,128)S(1)} %slice.427), kind=kLoop, calls=%fused_computation.56 | loop fusion | flops 10485760 | bytes 50331648 | tf_op jit(solution)/shard_map/add | solution.py:78
  236.8 9.3 %collective-permute-done.7 = f32[1024,128]{0,1:T(8,128)S(1)} collective-permute-done((f32[1024,128]{0,1:T(8,128)S(1)}, f32[1024,128]{0,1:T(8,128)S(1)}, u32[]{:S(2)}, u32[]{:S(2)}) %collective-permute-start.7) | collective-permute-done | bytes 524320 | tf_op jit(solution)/shard_map/ppermute | solution.py:18
  247.3 9.0 %pad_maximum_fusion.5 = f32[1024,2304]{0,1:T(8,128)} fusion(f32[1024,128]{0,1:T(8,128)S(1)} %collective-permute-done.7, f32[1024,2048]{0,1:T(8,128)} %bitcast.88, f32[1024,128]{0,1:T(8,128)S(1)} %collective-permute-done.6), kind=kLoop, calls=%fused_computation.7 | loop fusion | flops 4718592 | bytes 18874368 | tf_op jit(solution)/shard_map/concatenate | solution.py:19
  256.3 10.8 %fusion.2 = f32[1024,17,128]{0,2,1:T(8,128)} fusion(f32[1024,18,128]{0,2,1:T(8,128)} %bitcast.79, f32[17,128]{1,0:T(8,128)S(1)} %get-tuple-element.44, f32[17,128]{1,0:T(8,128)S(1)} %get-tuple-element.43), kind=kLoop, calls=%fused_computation.25 | loop fusion | flops 6684672 | bytes 26756096 | tf_op jit(solution)/shard_map/add | solution.py:34
  280.4 22.2 %fusion.18 = f32[1024,16,128]{0,2,1:T(8,128)} fusion(f32[1024,17,128]{0,2,1:T(8,128)} %fusion.2, f32[1024,16,128]{0,2,1:T(8,128)} %copy-done.8, f32[1024,16,127]{0,2,1:T(8,128)} %bitcast.95, f32[1024,16,1]{0,2,1:T(1,128)S(1)} %slice.438, f32[1024,16,128]{0,2,1:T(8,128)} %copy.20, f32[1024,16,128]{0,2,1:T(8,128)} %fusion.21), kind=kLoop, calls=%fused_computation.51 | loop fusion | flops 14680064 | bytes 58720256 | tf_op jit(solution)/shard_map/mul | solution.py:83
  302.6 9.2 %copy.22 = f32[1024,2048]{1,0:T(8,128)} copy(f32[1024,2048]{0,1:T(8,128)} %bitcast.103) | data formatting | bytes 16777216 | tf_op jit(solution)/shard_map/reshape | solution.py:57
  332.3 9.3 %copy.29 = f32[8,128,2048]{2,1,0:T(8,128)} copy(f32[8,128,2048]{1,0,2:T(8,128)} %bitcast.114) | data formatting | bytes 16777216 | tf_op jit(solution)/shard_map/reshape | solution.py:57
  358.5 11.8 %pad_maximum_fusion.6 = (f32[1152,2048]{1,0:T(8,128)}, f32[1152,2048]{1,0:T(8,128)}) fusion(f32[1024,2048]{1,0:T(8,128)} %copy-done.13, f32[128,2048]{1,0:T(8,128)S(1)} %collective-permute-done.8, f32[128,2048]{1,0:T(8,128)S(1)} %collective-permute-done.9), kind=kLoop, calls=%fused_computation.8 | loop fusion | flops 4718592 | bytes 29360128 | tf_op jit(solution)/shard_map/concatenate | solution.py:19
  370.3 11.1 %multiply_add_fusion.1 = f32[9,128,2048]{2,1,0:T(8,128)} fusion(f32[9,128,2048]{2,1,0:T(8,128)} %bitcast.108, f32[9,128,2048]{2,1,0:T(8,128)} %bitcast.107, f32[9,128]{1,0:T(8,128)S(1)} %get-tuple-element.40, f32[9,128]{1,0:T(8,128)S(1)} %get-tuple-element.39), kind=kLoop, calls=%fused_computation.15 | loop fusion | flops 7077888 | bytes 28320768 | tf_op jit(solution)/shard_map/add | solution.py:34
  381.4 17.5 %fusion.15 = f32[8,128,2048]{2,1,0:T(8,128)} fusion(f32[9,128,2048]{2,1,0:T(8,128)} %multiply_add_fusion.1, f32[8,128,2048]{2,1,0:T(8,128)} %copy-done.5, f32[8,127,2048]{2,1,0:T(8,128)} %bitcast.92, f32[8,1,2048]{2,1,0:T(1,128)S(1)} %slice.446, f32[8,128,2048]{2,1,0:T(8,128)} %copy.29, f32[8,128]{1,0:T(8,128)S(1)} %dynamic-slice_bitcast_fusion, ...), kind=kLoop, calls=%fused_computation.47 | loop fusion | flops 16777216 | bytes 50348032 | tf_op jit(solution)/shard_map/add | solution.py:78
  433.9 11.2 %multiply_add_fusion = f32[9,128,2048]{2,1,0:T(8,128)} fusion(f32[9,128,2048]{2,1,0:T(8,128)} %bitcast.110, f32[9,128,2048]{2,1,0:T(8,128)} %bitcast.109, f32[9,128]{1,0:T(8,128)S(1)} %get-tuple-element.40, f32[9,128]{1,0:T(8,128)S(1)} %get-tuple-element.39), kind=kLoop, calls=%fused_computation.14 | loop fusion | flops 7077888 | bytes 28320768 | tf_op jit(solution)/shard_map/add | solution.py:34
  445.0 22.1 %fusion.13 = f32[8,128,2048]{2,1,0:T(8,128)} fusion(f32[9,128,2048]{2,1,0:T(8,128)} %multiply_add_fusion, f32[8,128,2048]{2,1,0:T(8,128)} %copy-done.4, f32[8,127,2048]{2,1,0:T(8,128)} %bitcast.91, f32[8,1,2048]{2,1,0:T(1,128)S(1)} %slice.454, f32[8,128,2048]{2,1,0:T(8,128)} %fusion.15, f32[8,128,2048]{2,1,0:T(8,128)} %copy.29, ...), kind=kLoop, calls=%fused_computation.44 | loop fusion | flops 20971520 | bytes 58736640 | tf_op jit(solution)/shard_map/mul | solution.py:83
  467.1 9.3 %copy.23 = f32[1024,2048]{0,1:T(8,128)} copy(f32[1024,2048]{1,0:T(8,128)} %bitcast.99) | data formatting | bytes 16777216 | tf_op jit(solution)/shard_map/reshape | solution.py:56
  484.3 8.7 %copy.32 = f32[128,8,16,128]{3,2,1,0:T(8,128)} copy(f32[128,8,16,128]{3,1,2,0:T(8,128)} %bitcast.100) | data formatting | bytes 16777216
  501.8 9.0 %pad_maximum_fusion.10 = f32[1024,2304]{0,1:T(8,128)} fusion(f32[1024,128]{0,1:T(8,128)S(1)} %collective-permute-done.13, f32[1024,2048]{0,1:T(8,128)} %copy.23, f32[1024,128]{0,1:T(8,128)S(1)} %collective-permute-done.12), kind=kLoop, calls=%fused_computation.12 | loop fusion | flops 4718592 | bytes 18874368 | tf_op jit(solution)/shard_map/concatenate | solution.py:19
  511.8 8.9 %slice.463 = f32[1024,16,127]{0,2,1:T(8,128)} slice(f32[1024,18,128]{0,2,1:T(8,128)} %bitcast.76), slice={[0:1024], [1:17], [1:128]} | slice | bytes 16646144 | tf_op jit(solution)/shard_map/jit(_roll_static)/slice | solution.py:27
  530.9 21.3 %fusion.9 = f32[1024,16,128]{0,2,1:T(8,128)} fusion(f32[1024,16,128]{0,2,1:T(8,128)} %copy.27, f32[1024,17,128]{0,2,1:T(8,128)} %fusion.1, f32[1024,16,128]{0,2,1:T(8,128)} %copy-done.11, f32[1024,16,127]{0,2,1:T(8,128)} %bitcast.98, f32[1024,16,1]{0,2,1:T(1,128)S(1)} %slice.465), kind=kLoop, calls=%fused_computation.38 | loop fusion | flops 10485760 | bytes 50331648 | tf_op jit(solution)/shard_map/add | solution.py:78
  566.0 9.0 %pad_maximum_fusion.11 = f32[1024,2304]{0,1:T(8,128)} fusion(f32[1024,128]{0,1:T(8,128)S(1)} %collective-permute-done.15, f32[1024,2048]{0,1:T(8,128)} %bitcast.90, f32[1024,128]{0,1:T(8,128)S(1)} %collective-permute-done.14), kind=kLoop, calls=%fused_computation.13 | loop fusion | flops 4718592 | bytes 18874368 | tf_op jit(solution)/shard_map/concatenate | solution.py:19
  575.0 10.8 %fusion = f32[1024,17,128]{0,2,1:T(8,128)} fusion(f32[1024,18,128]{0,2,1:T(8,128)} %bitcast.83, f32[17,128]{1,0:T(8,128)S(1)} %get-tuple-element.36, f32[17,128]{1,0:T(8,128)S(1)} %get-tuple-element.35), kind=kLoop, calls=%fused_computation.19 | loop fusion | flops 6684672 | bytes 26756096 | tf_op jit(solution)/shard_map/add | solution.py:34
  599.1 22.2 %fusion.6 = f32[1024,16,128]{0,2,1:T(8,128)} fusion(f32[1024,17,128]{0,2,1:T(8,128)} %fusion, f32[1024,16,128]{0,2,1:T(8,128)} %copy-done.9, f32[1024,16,127]{0,2,1:T(8,128)} %bitcast.96, f32[1024,16,1]{0,2,1:T(1,128)S(1)} %slice.476, f32[1024,16,128]{0,2,1:T(8,128)} %copy.27, f32[1024,16,128]{0,2,1:T(8,128)} %fusion.9), kind=kLoop, calls=%fused_computation.33 | loop fusion | flops 14680064 | bytes 58720256 | tf_op jit(solution)/shard_map/mul | solution.py:83
  621.4 9.2 %copy.28 = f32[1024,2048]{1,0:T(8,128)} copy(f32[1024,2048]{0,1:T(8,128)} %bitcast.116) | data formatting | bytes 16777216 | tf_op jit(solution)/shard_map/reshape | solution.py:57
  (158 shorter events, 231.2 us)
Async XLA Ops:
  2.7 26.2 %collective-permute-start = (f32[128,2048]{1,0:T(8,128)}, f32[128,2048]{1,0:T(8,128)S(1)}, u32[]{:S(2)}, u32[]{:S(2)}) collective-permute-start(f32[128,2048]{1,0:T(8,128)} %get-tuple-element.27), channel_id=1, source_target_pairs={{0,4},{4,8},{8,12},{12,16},{16,20},{20,24},{24,28},{1,5},{5,9},{9,... | collective-permute-start | bytes 3145736 | tf_op jit(solution)/shard_map/ppermute | solution.py:17
  4.7 24.6 %collective-permute-start.1 = (f32[128,2048]{1,0:T(8,128)S(1)}, f32[128,2048]{1,0:T(8,128)S(1)}, u32[]{:S(2)}, u32[]{:S(2)}) collective-permute-start(f32[128,2048]{1,0:T(8,128)S(1)} %get-tuple-element.28), channel_id=1, source_target_pairs={{4,0},{8,4},{12,8},{16,12},{20,16},{24,20},{28,24},{5,1},{9,5},{13... | collective-permute-start | bytes 3145736 | tf_op jit(solution)/shard_map/ppermute | solution.py:18
  9.4 8.7 %copy-start.18 = (f32[2,64,128]{2,1,0:T(8,128)S(1)}, f32[2,64,128]{2,1,0:T(8,128)}, u32[]{:S(2)}) copy-start(f32[2,64,128]{2,1,0:T(8,128)} %param.6) | copy-start | bytes 196612
  18.8 10.1 %copy-start.19 = (f32[2,64,128]{2,1,0:T(8,128)S(1)}, f32[2,64,128]{2,1,0:T(8,128)}, u32[]{:S(2)}) copy-start(f32[2,64,128]{2,1,0:T(8,128)} %param.7) | copy-start | bytes 196612
  28.9 207.9 %copy-start.16 = (f32[64,128]{1,0:T(8,128)}, f32[64,128]{1,0:T(8,128)S(1)}, u32[]{:S(2)}) copy-start(f32[64,128]{1,0:T(8,128)S(1)} %get-tuple-element.31) | copy-start | bytes 98308
  73.3 14.0 %slice-start.2 = ((s8[8388608]{0:T(1024)(128)(4,1)}), s8[4194304]{0:T(1024)(128)(4,1)S(1)}, s32[]{:S(2)}) async-start(s8[8388608]{0:T(1024)(128)(4,1)} %bitcast.66), calls=%async_computation.2 | async-start | bytes 8388608
  75.2 17.1 %collective-permute-start.2 = (f32[128,2048]{1,0:T(8,128)S(1)}, f32[128,2048]{1,0:T(8,128)S(1)}, u32[]{:S(2)}, u32[]{:S(2)}) collective-permute-start(f32[128,2048]{1,0:T(8,128)S(1)} %get-tuple-element.23), channel_id=1, source_target_pairs={{0,4},{4,8},{8,12},{12,16},{16,20},{20,24},{24,28},{1,5},{5,9},{9,... | collective-permute-start | bytes 3145736 | tf_op jit(solution)/shard_map/ppermute | solution.py:17
  78.9 23.2 %collective-permute-start.3 = (f32[128,2048]{1,0:T(8,128)S(1)}, f32[128,2048]{1,0:T(8,128)}, u32[]{:S(2)}, u32[]{:S(2)}) collective-permute-start(f32[128,2048]{1,0:T(8,128)S(1)} %get-tuple-element.24), channel_id=1, source_target_pairs={{4,0},{8,4},{12,8},{16,12},{20,16},{24,20},{28,24},{5,1},{9,5},{13... | collective-permute-start | bytes 3145736 | tf_op jit(solution)/shard_map/ppermute | solution.py:18
  154.1 24.2 %collective-permute-start.5 = (f32[1024,128]{0,1:T(8,128)S(1)}, f32[1024,128]{0,1:T(8,128)S(1)}, u32[]{:S(2)}, u32[]{:S(2)}) collective-permute-start(f32[1024,128]{0,1:T(8,128)S(1)} %get-tuple-element.20), channel_id=1, source_target_pairs={{1,0},{2,1},{3,2},{5,4},{6,5},{7,6},{9,8},{10,9},{11,10},{13,12},{... | collective-permute-start | bytes 1572872 | tf_op jit(solution)/shard_map/ppermute | solution.py:18
  155.4 22.9 %collective-permute-start.4 = (f32[1024,128]{0,1:T(8,128)S(1)}, f32[1024,128]{0,1:T(8,128)S(1)}, u32[]{:S(2)}, u32[]{:S(2)}) collective-permute-start(f32[1024,128]{0,1:T(8,128)S(1)} %get-tuple-element.19), channel_id=1, source_target_pairs={{0,1},{1,2},{2,3},{4,5},{5,6},{6,7},{8,9},{9,10},{10,11},{12,13},{... | collective-permute-start | bytes 1572872 | tf_op jit(solution)/shard_map/ppermute | solution.py:17
  160.8 151.0 %copy-start.22 = (f32[1024]{0:T(1024)}, f32[1024]{0:T(1024)S(1)}, u32[]{:S(2)}) copy-start(f32[1024]{0:T(1024)S(1)} %dynamic_slice.31) | copy-start | bytes 12292
  188.3 8.9 %copy-start = (f32[1024,2304]{0,1:T(8,128)S(1)}, f32[1024,2304]{0,1:T(8,128)}, u32[]{:S(2)}) copy-start(f32[1024,2304]{0,1:T(8,128)} %pad_maximum_fusion.4) | copy-start | bytes 28311556
  230.0 16.1 %collective-permute-start.7 = (f32[1024,128]{0,1:T(8,128)S(1)}, f32[1024,128]{0,1:T(8,128)S(1)}, u32[]{:S(2)}, u32[]{:S(2)}) collective-permute-start(f32[1024,128]{0,1:T(8,128)S(1)} %get-tuple-element.18), channel_id=1, source_target_pairs={{1,0},{2,1},{3,2},{5,4},{6,5},{7,6},{9,8},{10,9},{11,10},{13,12},{... | collective-permute-start | bytes 1572872 | tf_op jit(solution)/shard_map/ppermute | solution.py:18
  231.3 16.0 %collective-permute-start.6 = (f32[1024,128]{0,1:T(8,128)S(1)}, f32[1024,128]{0,1:T(8,128)S(1)}, u32[]{:S(2)}, u32[]{:S(2)}) collective-permute-start(f32[1024,128]{0,1:T(8,128)S(1)} %get-tuple-element.17), channel_id=1, source_target_pairs={{0,1},{1,2},{2,3},{4,5},{5,6},{6,7},{8,9},{9,10},{10,11},{12,13},{... | collective-permute-start | bytes 1572872 | tf_op jit(solution)/shard_map/ppermute | solution.py:17
  236.1 75.8 %copy-start.24 = (s32[1024]{0:T(1024)}, s32[1024]{0:T(1024)S(1)}, u32[]{:S(2)}) copy-start(s32[1024]{0:T(1024)S(1)} %iota_add_fusion.1) | copy-start | bytes 12292
  256.3 12.0 %copy-start.2 = (f32[1024,2304]{0,1:T(8,128)S(1)}, f32[1024,2304]{0,1:T(8,128)}, u32[]{:S(2)}) copy-start(f32[1024,2304]{0,1:T(8,128)} %pad_maximum_fusion.5) | copy-start | bytes 28311556
  311.8 14.9 %copy-start.12 = (f32[1024,16,128]{0,2,1:T(8,128)S(1)}, f32[1024,16,128]{0,2,1:T(8,128)}, u32[]{:S(2)}) copy-start(f32[1024,16,128]{0,2,1:T(8,128)} %fusion.18) | copy-start | bytes 25165828
  320.8 37.7 %collective-permute-start.8 = (f32[128,2048]{1,0:T(8,128)}, f32[128,2048]{1,0:T(8,128)S(1)}, u32[]{:S(2)}, u32[]{:S(2)}) collective-permute-start(f32[128,2048]{1,0:T(8,128)} %get-tuple-element.15), channel_id=1, source_target_pairs={{0,4},{4,8},{8,12},{12,16},{16,20},{20,24},{24,28},{1,5},{5,9},{9,... | collective-permute-start | bytes 3145736 | tf_op jit(solution)/shard_map/ppermute | solution.py:17
  322.7 35.8 %collective-permute-start.9 = (f32[128,2048]{1,0:T(8,128)S(1)}, f32[128,2048]{1,0:T(8,128)S(1)}, u32[]{:S(2)}, u32[]{:S(2)}) collective-permute-start(f32[128,2048]{1,0:T(8,128)S(1)} %get-tuple-element.16), channel_id=1, source_target_pairs={{4,0},{8,4},{12,8},{16,12},{20,16},{24,20},{28,24},{5,1},{9,5},{13... | collective-permute-start | bytes 3145736 | tf_op jit(solution)/shard_map/ppermute | solution.py:18
  398.9 13.5 %slice-start = ((s8[8388608]{0:T(1024)(128)(4,1)}), s8[4194304]{0:T(1024)(128)(4,1)S(1)}, s32[]{:S(2)}) async-start(s8[8388608]{0:T(1024)(128)(4,1)} %bitcast.58), calls=%async_computation | async-start | bytes 8388608
  400.8 16.4 %collective-permute-start.10 = (f32[128,2048]{1,0:T(8,128)S(1)}, f32[128,2048]{1,0:T(8,128)S(1)}, u32[]{:S(2)}, u32[]{:S(2)}) collective-permute-start(f32[128,2048]{1,0:T(8,128)S(1)} %get-tuple-element.11), channel_id=1, source_target_pairs={{0,4},{4,8},{8,12},{12,16},{16,20},{20,24},{24,28},{1,5},{5,9},{9,... | collective-permute-start | bytes 3145736 | tf_op jit(solution)/shard_map/ppermute | solution.py:17
  402.7 23.0 %collective-permute-start.11 = (f32[128,2048]{1,0:T(8,128)S(1)}, f32[128,2048]{1,0:T(8,128)}, u32[]{:S(2)}, u32[]{:S(2)}) collective-permute-start(f32[128,2048]{1,0:T(8,128)S(1)} %get-tuple-element.12), channel_id=1, source_target_pairs={{4,0},{8,4},{12,8},{16,12},{20,16},{24,20},{28,24},{5,1},{9,5},{13... | collective-permute-start | bytes 3145736 | tf_op jit(solution)/shard_map/ppermute | solution.py:18
  467.1 17.1 %copy-start.15 = (f32[64,128]{1,0:T(8,128)S(1)}, f32[64,128]{1,0:T(8,128)}, u32[]{:S(2)}) copy-start(f32[64,128]{1,0:T(8,128)} %copy-done.14) | copy-start | bytes 98308
  467.1 17.2 %copy-start.17 = (f32[64,128]{1,0:T(8,128)S(1)}, f32[64,128]{1,0:T(8,128)}, u32[]{:S(2)}) copy-start(f32[64,128]{1,0:T(8,128)} %copy-done.16) | copy-start | bytes 98308
  477.7 24.1 %collective-permute-start.13 = (f32[1024,128]{0,1:T(8,128)S(1)}, f32[1024,128]{0,1:T(8,128)S(1)}, u32[]{:S(2)}, u32[]{:S(2)}) collective-permute-start(f32[1024,128]{0,1:T(8,128)S(1)} %get-tuple-element.8), channel_id=1, source_target_pairs={{1,0},{2,1},{3,2},{5,4},{6,5},{7,6},{9,8},{10,9},{11,10},{13,12},{... | collective-permute-start | bytes 1572872 | tf_op jit(solution)/shard_map/ppermute | solution.py:18
  479.0 22.8 %collective-permute-start.12 = (f32[1024,128]{0,1:T(8,128)S(1)}, f32[1024,128]{0,1:T(8,128)S(1)}, u32[]{:S(2)}, u32[]{:S(2)}) collective-permute-start(f32[1024,128]{0,1:T(8,128)S(1)} %get-tuple-element.7), channel_id=1, source_target_pairs={{0,1},{1,2},{2,3},{4,5},{5,6},{6,7},{8,9},{9,10},{10,11},{12,13},{... | collective-permute-start | bytes 1572872 | tf_op jit(solution)/shard_map/ppermute | solution.py:17
  511.8 8.9 %copy-start.1 = (f32[1024,2304]{0,1:T(8,128)S(1)}, f32[1024,2304]{0,1:T(8,128)}, u32[]{:S(2)}) copy-start(f32[1024,2304]{0,1:T(8,128)} %pad_maximum_fusion.10) | copy-start | bytes 28311556
  553.4 11.4 %collective-permute-start.15 = (f32[1024,128]{0,1:T(8,128)S(1)}, f32[1024,128]{0,1:T(8,128)S(1)}, u32[]{:S(2)}, u32[]{:S(2)}) collective-permute-start(f32[1024,128]{0,1:T(8,128)S(1)} %get-tuple-element.6), channel_id=1, source_target_pairs={{1,0},{2,1},{3,2},{5,4},{6,5},{7,6},{9,8},{10,9},{11,10},{13,12},{... | collective-permute-start | bytes 1572872 | tf_op jit(solution)/shard_map/ppermute | solution.py:18
  554.7 11.3 %collective-permute-start.14 = (f32[1024,128]{0,1:T(8,128)S(1)}, f32[1024,128]{0,1:T(8,128)S(1)}, u32[]{:S(2)}, u32[]{:S(2)}) collective-permute-start(f32[1024,128]{0,1:T(8,128)S(1)} %get-tuple-element.5), channel_id=1, source_target_pairs={{0,1},{1,2},{2,3},{4,5},{5,6},{6,7},{8,9},{9,10},{10,11},{12,13},{... | collective-permute-start | bytes 1572872 | tf_op jit(solution)/shard_map/ppermute | solution.py:17
  575.0 12.0 %copy-start.3 = (f32[1024,2304]{0,1:T(8,128)S(1)}, f32[1024,2304]{0,1:T(8,128)}, u32[]{:S(2)}) copy-start(f32[1024,2304]{0,1:T(8,128)} %pad_maximum_fusion.11) | copy-start | bytes 28311556
  621.3 9.2 %copy-start.23 = (f32[1024]{0:T(1024)S(1)}, f32[1024]{0:T(1024)}, u32[]{:S(2)}) copy-start(f32[1024]{0:T(1024)} %copy-done.22) | copy-start | bytes 12292
  621.3 9.2 %copy-start.25 = (s32[1024]{0:T(1024)S(1)}, s32[1024]{0:T(1024)}, u32[]{:S(2)}) copy-start(s32[1024]{0:T(1024)} %copy-done.24) | copy-start | bytes 12292
  (16 other events, 74.5 us)
where the time goes:
time: 646 us; the launch traced here: 637 us
  other arithmetic  367 us (57%)
  local copies, waits for them, and re-layouts  185 us (29%)
  starting transfers between devices  48.3 us (7%)
  waiting for transfers between devices  35.7 us (6%)
    mul x4, other arithmetic, heun_section(): return flatten(0.5 * (field + section_one + tend_two), lat_axis)  88.7 us
    add x4, other arithmetic, heun_section(): field + tendency(shaped(spread(matrix), lat_axis), east_here, faces_here,...  81.1 us
    concatenate x8, other arithmetic, extended_2(): array = jnp.concatenate([before, array, after], axis=dim)  75.9 us
    add x8, other arithmetic, tendency(): jnp.maximum(northern, 0.0) * below + jnp.minimum(northern, 0.0) * above  75 us
    slice x16, local copies, waits for them, and re-layouts, tendency(): eastward = jnp.roll(middle, -1, axis=lon_axis)  54.9 us
    unnamed x67, local copies, waits for them, and re-layouts  51.8 us
    ppermute x8, waiting for transfers between devices, extended_2(): after = lax.ppermute(first, axis, down)  33.3 us
    add x8, other arithmetic, tendency(): jnp.maximum(courant, 0.0) * middle + jnp.minimum(courant, 0.0) * eastward  31.1 us
  transfers between devices with their start and end apart: 16, of which 7 were waited for; matrix products, arithmetic and copies ran while one was open for 15% of the time, Pallas kernels for 0%

commit v1 on v0

v1 whole, which is shorter than its diff:
```python
import jax
import jax.numpy as jnp
from jax import lax
from jax.experimental import pallas as pl
from jax.experimental.pallas import tpu as pltpu
from jax.sharding import PartitionSpec as P

NLON = 128
CYCLES = 2
HALO = 2 * CYCLES


def coefficients(east, north):
    west = jnp.roll(east, 1, axis=-1)
    south = jnp.pad(north[:, :-1], ((0, 0), (1, 0), (0, 0)))
    up, down = (lambda v: jnp.maximum(v, 0.0)), (lambda v: jnp.minimum(v, 0.0))
    centre = 1.0 + ((down(west) - up(east)) + (down(south) - up(north)))
    to_north = -down(north)
    lines = north.shape[1]
    inside = (jnp.arange(lines) < lines - 1)[None, :, None]
    to_north = jnp.where(inside, to_north, 0.0)
    return jnp.stack([centre, -down(east), up(west), to_north, up(south)], axis=1)


def lines_of(coef, first, amount):
    padded = jnp.pad(coef, ((0, 0), (0, 0), (2 * HALO, 2 * HALO), (0, 0)))
    return lax.dynamic_slice_in_dim(padded, first + 2 * HALO, amount, 2)


def stencil(centre, east, west, north, south, c):
    return (c[0] * centre + (c[1] * east + c[2] * west)) + (c[3] * north + c[4] * south)


def row_kernel(lines, before_ref, mid_ref, after_ref, coef_ref, out_ref, one, two, three):
    total = lines + 2 * HALO
    width = 128

    def tile(j, carry):
        cols = pl.ds(pl.multiple_of(j * width, width), width)

        def source(l):
            if l < HALO:
                return before_ref[l * NLON:(l + 1) * NLON, cols]
            if l < HALO + lines:
                return mid_ref[(l - HALO) * NLON:(l - HALO + 1) * NLON, cols]
            l = l - HALO - lines
            return after_ref[l * NLON:(l + 1) * NLON, cols]

        def kept(ref):
            return lambda l: ref[l * NLON:(l + 1) * NLON, :]

        def step(read, l, cycle):
            c = [coef_ref[cycle * 5 + i, l * NLON:(l + 1) * NLON, :] for i in range(5)]
            g = read(l)
            return stencil(
                g, pltpu.roll(g, NLON - 1, 0), pltpu.roll(g, 1, 0), read(l + 1), read(l - 1), c
            )

        for l in range(1, total - 1):
            one[l * NLON:(l + 1) * NLON, :] = step(source, l, 0)
        for l in range(2, total - 2):
            two[l * NLON:(l + 1) * NLON, :] = 0.5 * (source(l) + step(kept(one), l, 0))
        for l in range(3, total - 3):
            three[l * NLON:(l + 1) * NLON, :] = step(kept(two), l, 1)
        for l in range(4, total - 4):
            value = 0.5 * (kept(two)(l) + step(kept(three), l, 1))
            out_ref[(l - HALO) * NLON:(l - HALO + 1) * NLON, cols] = value
        return carry

    lax.fori_loop(0, out_ref.shape[1] // width, tile, 0)


def row_sections(before, block, after, coef, rows, columns, chunk, tile):
    lines = rows // NLON
    total = rows + 2 * HALO * NLON
    per = columns // tile
    return pl.pallas_call(
        lambda *refs: row_kernel(lines, *refs),
        out_shape=jax.ShapeDtypeStruct((rows, columns), jnp.float32),
        grid=(per,),
        in_specs=[
            pl.BlockSpec((HALO * NLON, tile), lambda i: (0, i)),
            pl.BlockSpec((rows, tile), lambda i: (0, chunk * per + i)),
            pl.BlockSpec((HALO * NLON, tile), lambda i: (0, i)),
            pl.BlockSpec((5 * CYCLES, total, 128), lambda i: (0, 0, 0), pipeline_mode=pl.Buffered(1)),
        ],
        out_specs=pl.BlockSpec((rows, tile), lambda i: (0, i)),
        scratch_shapes=[pltpu.VMEM((total, 128), jnp.float32)] * 3,
        compiler_params=pltpu.CompilerParams(vmem_limit_bytes=40 << 20),
        cost_estimate=pl.CostEstimate(
            flops=60 * rows * columns, transcendentals=0, bytes_accessed=12 * rows * columns + (10 << 20)
        ),
        name="row_sections",
    )(before, block, after, coef)


def col_kernel(lines, chunks, sub, place_ref, *refs):
    before_ref, mids, after_ref = refs[0], refs[1:1 + chunks], refs[1 + chunks]
    coef_ref, noise_ref, out_ref, one, two, three = refs[2 + chunks:]
    total = lines + 2 * HALO
    each = lines // chunks
    row_line = place_ref[0] + pl.program_id(0) * out_ref.shape[0] // NLON
    shift = row_line - place_ref[1]

    def lane(l):
        return slice(l * NLON, (l + 1) * NLON)

    def part(j, carry):
        rows = pl.ds(pl.multiple_of(j * sub, sub), sub)

        def source(l):
            if l < HALO:
                return before_ref[rows, lane(l)]
            if l < HALO + lines:
                m, k = divmod(l - HALO, each)
                return mids[m][rows, lane(k)]
            return after_ref[rows, lane(l - HALO - lines)]

        def kept(ref):
            return lambda l: ref[:, lane(l)]

        def step(read, l, cycle):
            c = [
                jnp.broadcast_to(coef_ref[cycle * 5 + i:cycle * 5 + i + 1, lane(l)], (sub, NLON))
                for i in range(5)
            ]
            g = read(l)
            return stencil(
                g, pltpu.roll(g, NLON - 1, 1), pltpu.roll(g, 1, 1), read(l + 1), read(l - 1), c
            )

        for l in range(1, total - 1):
            one[:, lane(l)] = step(source, l, 0)
        for l in range(2, total - 2):
            two[:, lane(l)] = 0.5 * (source(l) + step(kept(one), l, 0))
        for d in range(5):
            at = shift + (d - 2 + HALO)

            @pl.when((at >= 2) & (at < total - 2))
            def _():
                cols = pl.ds(pl.multiple_of(at * NLON, NLON), NLON)
                two[:, cols] = two[:, cols] + noise_ref[rows, lane(d)]

        for l in range(3, total - 3):
            three[:, lane(l)] = step(kept(two), l, 1)
        for l in range(4, total - 4):
            out_ref[rows, lane(l - HALO)] = 0.5 * (kept(two)(l) + step(kept(three), l, 1))

        @pl.when((shift >= 0) & (shift < lines))
        def _():
            cols = pl.ds(pl.multiple_of(shift * NLON, NLON), NLON)
            out_ref[rows, cols] = out_ref[rows, cols] + noise_ref[rows, lane(5)]

        return carry

    lax.fori_loop(0, out_ref.shape[0] // sub, part, 0)


def col_sections(place, before, mids, after, coef, noise, rows, columns):
    lines, chunks, tile, sub = columns // NLON, len(mids), NLON, 32
    total = columns + 2 * HALO * NLON

    def rows_of(width):
        return pl.BlockSpec((tile, width), lambda i, s: (i, 0))

    return pl.pallas_call(
        lambda *refs: col_kernel(lines, chunks, sub, *refs),
        out_shape=jax.ShapeDtypeStruct((rows, columns), jnp.float32),
        grid_spec=pltpu.PrefetchScalarGridSpec(
            num_scalar_prefetch=1,
            grid=(rows // tile,),
            in_specs=[rows_of(HALO * NLON)]
            + [rows_of(columns // chunks)] * chunks
            + [
                rows_of(HALO * NLON),
                pl.BlockSpec((5 * CYCLES, total), lambda i, s: (0, 0), pipeline_mode=pl.Buffered(1)),
                rows_of(6 * NLON),
            ],
            out_specs=rows_of(columns),
            scratch_shapes=[pltpu.VMEM((sub, total), jnp.float32)] * 3,
        ),
        compiler_params=pltpu.CompilerParams(vmem_limit_bytes=40 << 20),
        cost_estimate=pl.CostEstimate(
            flops=60 * rows * columns, transcendentals=0, bytes_accessed=12 * rows * columns
        ),
        name="col_sections",
    )(place, before, *mids, after, coef, noise)


def spread_noise(coef, noise, first, lines):
    around = lines + 4
    c = lines_of(coef, first - 6, lines + 12)[1]
    padded = jnp.pad(noise.reshape(-1, NLON), ((2 * HALO, 2 * HALO), (0, 0)))
    mine = lax.dynamic_slice_in_dim(padded, first - 2 + 2 * HALO, around, 0)
    eye = jnp.eye(NLON, dtype=jnp.float32)
    centre = mine[:, :, None] * eye[None]
    field = jnp.pad(centre[:, None], ((0, 0), (4, 4), (0, 0), (0, 0)))
    factors = jnp.stack([c[:, k:k + around] for k in range(9)], axis=2)[..., None]

    def step(g):
        mid = g[:, 1:-1]
        trim = (9 - mid.shape[1]) // 2
        f = factors[:, :, trim:9 - trim]
        return stencil(
            mid, jnp.roll(mid, -1, axis=2), jnp.roll(mid, 1, axis=2), g[:, 2:], g[:, :-2], f
        )

    first_step = step(field)
    both = 0.5 * (field[:, 2:-2] + step(first_step))
    pieces = [both[d:d + lines, 4 - d] for d in range(5)] + [centre[2:2 + lines]]
    return jnp.concatenate([p.reshape(lines * NLON, NLON) for p in pieces], axis=1)


def on_device(covariance, model_noise, east_wind, north_wind):
    rows, columns = covariance.shape
    row_lines, col_lines = rows // NLON, columns // NLON
    edge = HALO * NLON
    row_first = lax.axis_index("row") * row_lines
    col_first = lax.axis_index("col") * col_lines
    row_size, col_size = lax.axis_size("row"), lax.axis_size("col")
    row_up = [(i, i + 1) for i in range(row_size - 1)]
    row_down = [(j, i) for i, j in row_up]
    col_up = [(i, i + 1) for i in range(col_size - 1)]
    col_down = [(j, i) for i, j in col_up]

    chunks = columns // edge
    order = [0, chunks - 1] + list(range(1, chunks - 1))
    halos = {}
    for k in order:
        part = covariance[:, k * edge:(k + 1) * edge]
        halos[k] = (
            lax.ppermute(part[rows - edge:], "row", row_up),
            lax.ppermute(part[:edge], "row", row_down),
        )

    coef = coefficients(east_wind, north_wind)
    row_coef = lines_of(coef, row_first - HALO, row_lines + 2 * HALO).reshape(5 * CYCLES, -1)
    row_coef = jnp.broadcast_to(row_coef[:, :, None], row_coef.shape + (128,))
    col_coef = lines_of(coef, col_first - HALO, col_lines + 2 * HALO).reshape(5 * CYCLES, -1)
    noise = spread_noise(coef, model_noise, row_first, row_lines)

    mids = {}
    for k in order:
        mids[k] = row_sections(
            halos[k][0], covariance, halos[k][1], row_coef, rows, edge, k, min(256, edge)
        )
    after = lax.ppermute(mids[0], "col", col_down)
    before = lax.ppermute(mids[chunks - 1], "col", col_up)
    place = jnp.stack([row_first, col_first]).astype(jnp.int32)
    return col_sections(
        place, before, [mids[k] for k in range(chunks)], after, col_coef, noise, rows, columns
    )


def solution(mesh):
    in_specs = (P("row", "col"), P(), P(), P())
    out_specs = P("row", "col")
    return jax.shard_map(
        on_device, mesh=mesh, in_specs=in_specs, out_specs=out_specs, check_vma=False
    )
```

time: 646 us -> 170 us (0.26)
  other arithmetic: 367 us -> 23 us
  local copies, waits for them, and re-layouts: 185 us -> 34.8 us
  Pallas kernels: 0 us -> 73.2 us
  waiting for transfers between devices: 35.7 us -> 6.92 us
  starting transfers between devices: 48.3 us -> 28.3 us
    add x26 -> x1, other arithmetic: 202 us -> 12.3 us  [stencil(): c[0] * centre + (c[1] * east + c[2] * west) + (c[3] * north + c[4] * south)]
    mul x4 -> x3, other arithmetic: 88.7 us -> 9.48 us  [the longest x1 9.02 us: spread_noise(): both = 0.5 * (field[:, 2:-2] + step(first_step))]
    concatenate x8 -> x0, other arithmetic: 75.9 us -> none  [extended_2(): array = jnp.concatenate([before, array, after], axis=dim)]
    pallas_call x0 -> x5, Pallas kernels: none -> 73.2 us  [the longest x4 43.4 us: row_sections(): pl.pallas_call(lambda *refs: row_kernel(lines, *refs), out_shape=jax.Shap...]
    slice x32 -> x7, local copies, waits for them, and re-layouts: 68.3 us -> 18 us  [the longest x4 10.8 us: step(): jnp.roll(mid, 1, axis=2)]
    reshape x5 -> x0, local copies, waits for them, and re-layouts: 46.3 us -> none  [the longest x3 27.7 us: flatten(): return field.reshape(field.shape[0], field.shape[1] * NLON)]
    unnamed x67 -> x49, local copies, waits for them, and re-layouts: 51.8 us -> 7.97 us
    ppermute x16 -> x10, waiting for transfers between devices: 35.7 us -> 6.92 us  [the longest x1 6.89 us: on_device(): before = lax.ppermute(mids[chunks - 1], 'col', col_up)]
  transfers between devices with their start and end apart: 16 -> 10, of which waited for: 7 -> 1; matrix products, arithmetic and copies ran while one was open for 15% -> 26% of each run, Pallas kernels for 0% -> 26%
where the time goes in v1:
time: 170 us; the launch traced here: 167 us
  Pallas kernels  73.2 us (43%)
  local copies, waits for them, and re-layouts  34.8 us (20%)
  starting transfers between devices  28.3 us (17%)
  other arithmetic  23 us (14%)
  waiting for transfers between devices  6.92 us (4%)
    pallas_call x4, Pallas kernels, row_sections(): pl.pallas_call(lambda *refs: row_kernel(lines, *refs), out_shape=jax.Shap...  43.4 us
    pallas_call x1, Pallas kernels, col_sections(): pl.pallas_call(lambda *refs: col_kernel(lines, chunks, sub, *refs), out_s...  29.8 us
    add x1, other arithmetic, stencil(): c[0] * centre + (c[1] * east + c[2] * west) + (c[3] * north + c[4] * south)  12.3 us
    ppermute x4, starting transfers between devices, on_device(): lax.ppermute(part[:edge], 'row', row_down)  12.3 us
    slice x4, local copies, waits for them, and re-layouts, step(): jnp.roll(mid, 1, axis=2)  10.8 us
    ppermute x4, starting transfers between devices, on_device(): lax.ppermute(part[rows - edge:], 'row', row_up)  10.1 us
    mul x1, other arithmetic, spread_noise(): both = 0.5 * (field[:, 2:-2] + step(first_step))  9.02 us
    unnamed x49, local copies, waits for them, and re-layouts  7.97 us
  transfers between devices with their start and end apart: 10, of which 1 were waited for; matrix products, arithmetic and copies ran while one was open for 26% of the time, Pallas kernels for 26%

profile of v1, /device:TPU:2, one launch (start us, length us, event | category | flops | bytes accessed | tf_op | source)
XLA Modules:
  0.0 166.9 jit_solution(17666568061610018811)
XLA Ops:
  0.0 7.0 %fusion.21 = (f32[512,512]{1,0:T(8,128)}, f32[512,512]{1,0:T(8,128)}, f32[512,512]{1,0:T(8,128)}, f32[512,512]{1,0:T(8,128)}, f32[512,512]{1,0:T(8,128)}, /*inde...) fusion(f32[1024,2048]{1,0:T(8,128)} %refs_1_.7), kind=kLoop, calls=%fused_computation.86 | loop fusion | bytes 16777216 | tf_op jit(solution)/shard_map/slice | solution.py:233
  7.0 1.9 %collective-permute-start.3 = (f32[512,512]{1,0:T(8,128)}, f32[512,512]{1,0:T(8,128)S(1)}, u32[]{:S(2)}, u32[]{:S(2)}) collective-permute-start(f32[512,512]{1,0:T(8,128)} %get-tuple-element.10), channel_id=1, source_target_pairs={{0,4},{4,8},{8,12},{12,16},{16,20},{20,24},{24,28},{1,5},{5,9},{9,... | collective-permute-start | bytes 3145736 | tf_op jit(solution)/shard_map/ppermute | solution.py:232
  8.9 3.6 %collective-permute-start.4 = (f32[512,512]{1,0:T(8,128)}, f32[512,512]{1,0:T(8,128)}, u32[]{:S(2)}, u32[]{:S(2)}) collective-permute-start(f32[512,512]{1,0:T(8,128)} %get-tuple-element.9), channel_id=1, source_target_pairs={{4,0},{8,4},{12,8},{16,12},{20,16},{24,20},{28,24},{5,1},{9,5},{13... | collective-permute-start | bytes 3145736 | tf_op jit(solution)/shard_map/ppermute | solution.py:233
  12.6 1.9 %collective-permute-start = (f32[512,512]{1,0:T(8,128)}, f32[512,512]{1,0:T(8,128)}, u32[]{:S(2)}, u32[]{:S(2)}) collective-permute-start(f32[512,512]{1,0:T(8,128)} %get-tuple-element.12), channel_id=1, source_target_pairs={{0,4},{4,8},{8,12},{12,16},{16,20},{20,24},{24,28},{1,5},{5,9},{9,... | collective-permute-start | bytes 3145736 | tf_op jit(solution)/shard_map/ppermute | solution.py:232
  14.5 3.6 %collective-permute-start.1 = (f32[512,512]{1,0:T(8,128)}, f32[512,512]{1,0:T(8,128)}, u32[]{:S(2)}, u32[]{:S(2)}) collective-permute-start(f32[512,512]{1,0:T(8,128)} %get-tuple-element.11), channel_id=1, source_target_pairs={{4,0},{8,4},{12,8},{16,12},{20,16},{24,20},{28,24},{5,1},{9,5},{13... | collective-permute-start | bytes 3145736 | tf_op jit(solution)/shard_map/ppermute | solution.py:233
  18.1 2.7 %collective-permute-start.5 = (f32[512,512]{1,0:T(8,128)}, f32[512,512]{1,0:T(8,128)S(1)}, u32[]{:S(2)}, u32[]{:S(2)}) collective-permute-start(f32[512,512]{1,0:T(8,128)} %get-tuple-element.8), channel_id=1, source_target_pairs={{0,4},{4,8},{8,12},{12,16},{16,20},{20,24},{24,28},{1,5},{5,9},{9,... | collective-permute-start | bytes 3145736 | tf_op jit(solution)/shard_map/ppermute | solution.py:232
  20.8 0.7 slice_bitcast_fusion.20
  23.1 5.5 %pad_slice_fusion.2 = (f32[12,7,127,128]{3,2,0,1:T(8,128)}, f32[12,7,127,128]{3,2,0,1:T(8,128)}) fusion(f32[12,1,128,128]{3,2,0,1:T(8,128)S(1)} %broadcast_multiply_fusion), kind=kLoop, calls=%fused_computation.2 | loop fusion | bytes 11710464 | tf_op jit(solution)/shard_map/jit(_roll_static)/slice | solution.py:205
  28.7 0.7 pad_slice_fusion.3
  29.3 1.0 fusion.17
  30.7 0.8 copy-done.8
  31.5 0.7 slice_bitcast_fusion.4
  32.3 12.3 %fusion.2 = f32[12,7,128,128]{3,2,0,1:T(8,128)S(1)} fusion(f32[12,1,128,128]{3,2,0,1:T(8,128)S(1)} %broadcast_multiply_fusion, f32[12,7,1,128]{3,2,0,1:T(1,128)} %get-tuple-element.23, f32[12,7,127,128]{3,2,0,1:T(8,128)} %get-tuple-element.25, f32[12,7,127,128]{3,2,0,1:T(8,128)} %get-tuple-element.24, f32[12,7,1,128]{3,2,0,1:T(1,128)} %get-tuple-element.22, ...), kind=kLoop, calls=%fused_computation.10 | loop fusion | flops 15138816 | bytes 17516544 | tf_op jit(solution)/shard_map/add | solution.py:31
  45.4 4.5 %fusion.23 = (f32[12,5,127,128]{3,2,0,1:T(8,128)}, f32[12,5,127,128]{3,2,0,1:T(8,128)}) fusion(f32[12,7,128,128]{3,2,0,1:T(8,128)S(1)} %fusion.2), kind=kLoop, calls=%fused_computation.88 | loop fusion | bytes 15605760 | tf_op jit(solution)/shard_map/jit(_roll_static)/slice | solution.py:205
  50.0 1.3 copy-done.4
  51.3 1.0 copy-done
  52.2 2.9 %collective-permute-start.6 = (f32[512,512]{1,0:T(8,128)}, f32[512,512]{1,0:T(8,128)S(1)}, u32[]{:S(2)}, u32[]{:S(2)}) collective-permute-start(f32[512,512]{1,0:T(8,128)} %get-tuple-element.7), channel_id=1, source_target_pairs={{4,0},{8,4},{12,8},{16,12},{20,16},{24,20},{28,24},{5,1},{9,5},{13... | collective-permute-start | bytes 3145736 | tf_op jit(solution)/shard_map/ppermute | solution.py:233
  55.1 3.6 %collective-permute-start.7 = (f32[512,512]{1,0:T(8,128)}, f32[512,512]{1,0:T(8,128)S(1)}, u32[]{:S(2)}, u32[]{:S(2)}) collective-permute-start(f32[512,512]{1,0:T(8,128)} %get-tuple-element.6), channel_id=1, source_target_pairs={{0,4},{4,8},{8,12},{12,16},{16,20},{20,24},{24,28},{1,5},{5,9},{9,... | collective-permute-start | bytes 3145736 | tf_op jit(solution)/shard_map/ppermute | solution.py:232
  58.7 5.9 %broadcast_in_dim.26.refs_3_ = f32[10,2048,128]{2,1,0:T(8,128)} broadcast(f32[10,2048]{1,0:T(8,128)S(1)} %bitcast.106), dimensions={0,1} | broadcast | bytes 10567680 | tf_op jit(solution)/shard_map/broadcast_in_dim | solution.py:238
  64.7 10.9 %row_sections.5.refs_2_ = f32[1024,512]{1,0:T(8,128)S(1)} custom-call(f32[512,512]{1,0:T(8,128)S(1)} %copy-done.1, f32[1024,2048]{1,0:T(8,128)S(1)} %bitcast.92, f32[512,512]{1,0:T(8,128)} %collective-permute-done.4.refs_2_, f32[10,2048,128]{2,1,0:T(8,128)} %broadcast_in_dim.26.refs_3_), custom_call_target="tpu_custom_call" | custom-call | flops 31457280 | bytes 16777216 | tf_op jit(solution)/shard_map/row_sections/pallas_call | solution.py:77
  75.6 1.3 collective-permute-start.9
  76.9 11.0 %row_sections.4.refs_5_ = f32[1024,512]{1,0:T(8,128)S(1)} custom-call(f32[512,512]{1,0:T(8,128)} %collective-permute-done.refs_0_, f32[1024,2048]{1,0:T(8,128)S(1)} %bitcast.92, f32[512,512]{1,0:T(8,128)} %collective-permute-done.1.refs_2_, f32[10,2048,128]{2,1,0:T(8,128)} %broadcast_in_dim.26.refs_3_), custom_call_target="tpu_custom_call" | custom-call | flops 31457280 | bytes 16777216 | tf_op jit(solution)/shard_map/row_sections/pallas_call | solution.py:77
  87.9 4.7 %collective-permute-start.2 = (f32[1024,512]{1,0:T(8,128)S(1)}, f32[1024,512]{1,0:T(8,128)S(1)}, u32[]{:S(2)}, u32[]{:S(2)}) collective-permute-start(f32[1024,512]{1,0:T(8,128)S(1)} %row_sections.4.refs_5_), channel_id=1, source_target_pairs={{0,1},{1,2},{2,3},{4,5},{5,6},{6,7},{8,9},{9,10},{10,11},{12,13},{... | collective-permute-start | bytes 6291464 | tf_op jit(solution)/shard_map/ppermute | solution.py:248
  92.6 9.0 %fusion.8 = f32[12,5,128,128]{3,2,0,1:T(8,128)S(1)} fusion(f32[12,1,128,128]{3,2,0,1:T(8,128)S(1)} %broadcast_multiply_fusion, f32[12,7,128,128]{3,2,0,1:T(8,128)} %copy-done.4, f32[12,5,1,128]{3,2,0,1:T(1,128)S(1)} %get-tuple-element.14, f32[12,5,127,128]{3,2,0,1:T(8,128)} %get-tuple-element.16, f32[12,5,127,128]{3,2,0,1:T(8,128)} %get-tuple-element.15, ...), kind=kLoop, calls=%fused_computation.18 | loop fusion | flops 12779520 | bytes 24532992 | tf_op jit(solution)/shard_map/mul | solution.py:209
  101.9 2.1 %collective-permute-start.8 = (f32[512,512]{1,0:T(8,128)}, f32[512,512]{1,0:T(8,128)S(1)}, u32[]{:S(2)}, u32[]{:S(2)}) collective-permute-start(f32[512,512]{1,0:T(8,128)} %get-tuple-element.5), channel_id=1, source_target_pairs={{4,0},{8,4},{12,8},{16,12},{20,16},{24,20},{28,24},{5,1},{9,5},{13... | collective-permute-start | bytes 3145736 | tf_op jit(solution)/shard_map/ppermute | solution.py:233
  104.7 1.7 %copy-done.5 = f32[1024,768]{1,0:T(8,128)} copy-done((f32[1024,768]{1,0:T(8,128)}, f32[1024,768]{1,0:T(8,128)S(1)}, u32[]{:S(2)}) %copy-start.5) | copy-done | bytes 3145752
  106.4 10.8 %row_sections.6.refs_3_ = f32[1024,512]{1,0:T(8,128)S(1)} custom-call(f32[512,512]{1,0:T(8,128)S(1)} %collective-permute-done.5.refs_0_, f32[1024,2048]{1,0:T(8,128)S(1)} %bitcast.92, f32[512,512]{1,0:T(8,128)S(1)} %collective-permute-done.6.refs_2_, f32[10,2048,128]{2,1,0:T(8,128)} %broadcast_in_dim.26.refs_3_), custom_call_target="tpu_custom_call" | custom-call | flops 31457280 | bytes 16777216 | tf_op jit(solution)/shard_map/row_sections/pallas_call | solution.py:77
  117.2 1.0 copy-done.2
  118.2 1.2 copy-done.3
  119.4 10.8 %row_sections.7.refs_4_ = f32[1024,512]{1,0:T(8,128)S(1)} custom-call(f32[512,512]{1,0:T(8,128)S(1)} %collective-permute-done.7.refs_0_, f32[1024,2048]{1,0:T(8,128)S(1)} %bitcast.92, f32[512,512]{1,0:T(8,128)S(1)} %copy-done.3, f32[10,2048,128]{2,1,0:T(8,128)} %broadcast_in_dim.26.refs_3_), custom_call_target="tpu_custom_call" | custom-call | flops 31457280 | bytes 16777216 | tf_op jit(solution)/shard_map/row_sections/pallas_call | solution.py:77
  130.2 6.9 %collective-permute-done.2.refs_1_ = f32[1024,512]{1,0:T(8,128)S(1)} collective-permute-done((f32[1024,512]{1,0:T(8,128)S(1)}, f32[1024,512]{1,0:T(8,128)S(1)}, u32[]{:S(2)}, u32[]{:S(2)}) %collective-permute-start.2) | collective-permute-done | bytes 2097184 | tf_op jit(solution)/shard_map/ppermute | solution.py:248
  137.1 29.8 %col_sections.1 = f32[1024,2048]{1,0:T(8,128)} custom-call(s32[2]{0:T(128)S(1)} %pad_add_fusion.refs_0_, f32[1024,512]{1,0:T(8,128)S(1)} %collective-permute-done.2.refs_1_, f32[1024,512]{1,0:T(8,128)S(1)} %row_sections.5.refs_2_, f32[1024,512]{1,0:T(8,128)S(1)} %row_sections.6.refs_3_, f32[1024,512]{1,0:T(8,128)S(1)} %row_sections.7.refs_4_, ...), custom_call_target="tpu_custom_call" | custom-call | flops 125829120 | bytes 25165824 | tf_op jit(solution)/shard_map/col_sections/pallas_call | solution.py:166
  (75 shorter events, 3.5 us)
Async XLA Ops:
  0.0 20.8 %copy-start.6 = (f32[2,64,128]{2,1,0:T(8,128)S(1)}, f32[2,64,128]{2,1,0:T(8,128)}, u32[]{:S(2)}) copy-start(f32[2,64,128]{2,1,0:T(8,128)} %param.6) | copy-start | bytes 196612
  0.0 22.2 %copy-start.13 = (f32[8192]{0:T(1024)S(1)}, f32[8192]{0:T(1024)}, u32[]{:S(2)}) copy-start(f32[8192]{0:T(1024)} %param.5) | copy-start | bytes 98308
  7.0 43.0 %collective-permute-start.3 = (f32[512,512]{1,0:T(8,128)}, f32[512,512]{1,0:T(8,128)S(1)}, u32[]{:S(2)}, u32[]{:S(2)}) collective-permute-start(f32[512,512]{1,0:T(8,128)} %get-tuple-element.10), channel_id=1, source_target_pairs={{0,4},{4,8},{8,12},{12,16},{16,20},{20,24},{24,28},{1,5},{5,9},{9,... | collective-permute-start | bytes 3145736 | tf_op jit(solution)/shard_map/ppermute | solution.py:232
  8.9 46.2 %collective-permute-start.4 = (f32[512,512]{1,0:T(8,128)}, f32[512,512]{1,0:T(8,128)}, u32[]{:S(2)}, u32[]{:S(2)}) collective-permute-start(f32[512,512]{1,0:T(8,128)} %get-tuple-element.9), channel_id=1, source_target_pairs={{4,0},{8,4},{12,8},{16,12},{20,16},{24,20},{28,24},{5,1},{9,5},{13... | collective-permute-start | bytes 3145736 | tf_op jit(solution)/shard_map/ppermute | solution.py:233
  12.6 63.1 %collective-permute-start = (f32[512,512]{1,0:T(8,128)}, f32[512,512]{1,0:T(8,128)}, u32[]{:S(2)}, u32[]{:S(2)}) collective-permute-start(f32[512,512]{1,0:T(8,128)} %get-tuple-element.12), channel_id=1, source_target_pairs={{0,4},{4,8},{8,12},{12,16},{16,20},{20,24},{24,28},{1,5},{5,9},{9,... | collective-permute-start | bytes 3145736 | tf_op jit(solution)/shard_map/ppermute | solution.py:232
  14.5 62.4 %collective-permute-start.1 = (f32[512,512]{1,0:T(8,128)}, f32[512,512]{1,0:T(8,128)}, u32[]{:S(2)}, u32[]{:S(2)}) collective-permute-start(f32[512,512]{1,0:T(8,128)} %get-tuple-element.11), channel_id=1, source_target_pairs={{4,0},{8,4},{12,8},{16,12},{20,16},{24,20},{28,24},{5,1},{9,5},{13... | collective-permute-start | bytes 3145736 | tf_op jit(solution)/shard_map/ppermute | solution.py:233
  18.1 83.8 %collective-permute-start.5 = (f32[512,512]{1,0:T(8,128)}, f32[512,512]{1,0:T(8,128)S(1)}, u32[]{:S(2)}, u32[]{:S(2)}) collective-permute-start(f32[512,512]{1,0:T(8,128)} %get-tuple-element.8), channel_id=1, source_target_pairs={{0,4},{4,8},{8,12},{12,16},{16,20},{20,24},{24,28},{1,5},{5,9},{9,... | collective-permute-start | bytes 3145736 | tf_op jit(solution)/shard_map/ppermute | solution.py:232
  22.2 0.6 copy-start.11
  23.1 6.2 %copy-start.7 = (f32[2,64,128]{2,1,0:T(8,128)S(1)}, f32[2,64,128]{2,1,0:T(8,128)}, u32[]{:S(2)}) copy-start(f32[2,64,128]{2,1,0:T(8,128)} %param.7) | copy-start | bytes 196612
  30.7 0.8 copy-start.8
  32.3 13.0 %copy-start.9 = (f32[5,12,9,128]{3,1,0,2:T(8,128)S(1)}, f32[5,12,9,128]{3,1,0,2:T(8,128)}, u32[]{:S(2)}) copy-start(f32[5,12,9,128]{3,1,0,2:T(8,128)} %copy-done.8) | copy-start | bytes 829444
  44.7 6.6 %copy-start.4 = (f32[12,7,128,128]{3,2,0,1:T(8,128)}, f32[12,7,128,128]{3,2,0,1:T(8,128)S(1)}, u32[]{:S(2)}) copy-start(f32[12,7,128,128]{3,2,0,1:T(8,128)S(1)} %fusion.2) | copy-start | bytes 16515076
  44.7 20.0 %slice-start = ((s8[8388608]{0:T(1024)(128)(4,1)}), s8[4194304]{0:T(1024)(128)(4,1)S(1)}, s32[]{:S(2)}) async-start(s8[8388608]{0:T(1024)(128)(4,1)} %bitcast.91), calls=%async_computation | async-start | bytes 8388608
  45.4 19.2 %slice-start.1 = ((s8[8388608]{0:T(1024)(128)(4,1)}), s8[4194304]{0:T(1024)(128)(4,1)S(1)}, s32[]{:S(2)}) async-start(s8[8388608]{0:T(1024)(128)(4,1)} %bitcast.91), calls=%async_computation.1 | async-start | bytes 8388608
  51.3 1.0 copy-start
  52.2 54.2 %collective-permute-start.6 = (f32[512,512]{1,0:T(8,128)}, f32[512,512]{1,0:T(8,128)S(1)}, u32[]{:S(2)}, u32[]{:S(2)}) collective-permute-start(f32[512,512]{1,0:T(8,128)} %get-tuple-element.7), channel_id=1, source_target_pairs={{4,0},{8,4},{12,8},{16,12},{20,16},{24,20},{28,24},{5,1},{9,5},{13... | collective-permute-start | bytes 3145736 | tf_op jit(solution)/shard_map/ppermute | solution.py:233
  55.1 62.1 %collective-permute-start.7 = (f32[512,512]{1,0:T(8,128)}, f32[512,512]{1,0:T(8,128)S(1)}, u32[]{:S(2)}, u32[]{:S(2)}) collective-permute-start(f32[512,512]{1,0:T(8,128)} %get-tuple-element.6), channel_id=1, source_target_pairs={{0,4},{4,8},{8,12},{12,16},{16,20},{20,24},{24,28},{1,5},{5,9},{9,... | collective-permute-start | bytes 3145736 | tf_op jit(solution)/shard_map/ppermute | solution.py:232
  58.7 6.0 %copy-start.1 = (f32[512,512]{1,0:T(8,128)S(1)}, f32[512,512]{1,0:T(8,128)}, u32[]{:S(2)}) copy-start(f32[512,512]{1,0:T(8,128)} %copy-done) | copy-start | bytes 3145732
  75.6 54.6 %collective-permute-start.9 = (f32[1024,512]{1,0:T(8,128)S(1)}, f32[1024,512]{1,0:T(8,128)S(1)}, u32[]{:S(2)}, u32[]{:S(2)}) collective-permute-start(f32[1024,512]{1,0:T(8,128)S(1)} %row_sections.5.refs_2_), channel_id=1, source_target_pairs={{1,0},{2,1},{3,2},{5,4},{6,5},{7,6},{9,8},{10,9},{11,10},{13,12},{... | collective-permute-start | bytes 6291464 | tf_op jit(solution)/shard_map/ppermute | solution.py:247
  87.9 49.2 %collective-permute-start.2 = (f32[1024,512]{1,0:T(8,128)S(1)}, f32[1024,512]{1,0:T(8,128)S(1)}, u32[]{:S(2)}, u32[]{:S(2)}) collective-permute-start(f32[1024,512]{1,0:T(8,128)S(1)} %row_sections.4.refs_5_), channel_id=1, source_target_pairs={{0,1},{1,2},{2,3},{4,5},{5,6},{6,7},{8,9},{9,10},{10,11},{12,13},{... | collective-permute-start | bytes 6291464 | tf_op jit(solution)/shard_map/ppermute | solution.py:248
  101.7 2.5 %copy-start.12 = (f32[12,128]{1,0:T(8,128)S(1)}, f32[12,128]{1,0:T(8,128)}, u32[]{:S(2)}) copy-start(f32[12,128]{1,0:T(8,128)} %copy-done.11) | copy-start | bytes 18436
  101.7 2.5 %copy-start.10 = (f32[2,5,24,128]{3,2,0,1:T(8,128)S(1)}, f32[2,5,24,128]{3,2,0,1:T(8,128)}, u32[]{:S(2)}) copy-start(f32[2,5,24,128]{3,2,0,1:T(8,128)} %pad_dynamic-slice_fusion.1) | copy-start | bytes 368644
  101.9 15.3 %collective-permute-start.8 = (f32[512,512]{1,0:T(8,128)}, f32[512,512]{1,0:T(8,128)S(1)}, u32[]{:S(2)}, u32[]{:S(2)}) collective-permute-start(f32[512,512]{1,0:T(8,128)} %get-tuple-element.5), channel_id=1, source_target_pairs={{4,0},{8,4},{12,8},{16,12},{20,16},{24,20},{28,24},{5,1},{9,5},{13... | collective-permute-start | bytes 3145736 | tf_op jit(solution)/shard_map/ppermute | solution.py:233
  104.7 1.8 %copy-start.5 = (f32[1024,768]{1,0:T(8,128)}, f32[1024,768]{1,0:T(8,128)S(1)}, u32[]{:S(2)}) copy-start(f32[1024,768]{1,0:T(8,128)S(1)} %constant_dynamic-update-slice_fusion.9.refs_8_) | copy-start | bytes 9437188
  117.2 1.0 copy-start.2
  118.2 1.2 copy-start.3

commit v2 on v0

v2 whole, which is shorter than its diff:
```python
import jax
import jax.numpy as jnp
from jax import lax
from jax.experimental import pallas as pl
from jax.experimental.pallas import tpu as pltpu
from jax.sharding import PartitionSpec as P

NLON = 128
CYCLES = 2
HALO = 2 * CYCLES


def coefficients(east, north):
    west = jnp.roll(east, 1, axis=-1)
    south = jnp.pad(north[:, :-1], ((0, 0), (1, 0), (0, 0)))
    up, down = (lambda v: jnp.maximum(v, 0.0)), (lambda v: jnp.minimum(v, 0.0))
    centre = 1.0 + ((down(west) - up(east)) + (down(south) - up(north)))
    to_north = -down(north)
    lines = north.shape[1]
    inside = (jnp.arange(lines) < lines - 1)[None, :, None]
    to_north = jnp.where(inside, to_north, 0.0)
    return jnp.stack([centre, -down(east), up(west), to_north, up(south)], axis=1)


def lines_of(coef, first, amount):
    padded = jnp.pad(coef, ((0, 0), (0, 0), (2 * HALO, 2 * HALO), (0, 0)))
    return lax.dynamic_slice_in_dim(padded, first + 2 * HALO, amount, 2)


def shifted(values, step):
    lines, lons = step
    if lines > 0:
        values = jnp.pad(values[lines:], ((0, lines), (0, 0)))
    elif lines < 0:
        values = jnp.pad(values[:lines], ((-lines, 0), (0, 0)))
    return jnp.roll(values, -lons, axis=1) if lons else values


REACH = [(-2, 0), (-1, -1), (-1, 0), (-1, 1), (0, -2), (0, -1), (0, 0), (0, 1), (0, 2), (1, -1), (1, 0), (1, 1), (2, 0)]


def spread_noise(coef, noise, scale):
    steps = [(0, 0), (0, 1), (0, -1), (1, 0), (-1, 0)]
    once = [coef[i] - 1.0 if i == 0 else coef[i] for i in range(5)]
    weights = {r: 0.0 for r in REACH}
    weights[(0, 0)] = 1.0
    for p, a in zip(steps, once):
        weights[p] = weights[p] + a
        for q, b in zip(steps, once):
            at = (p[0] + q[0], p[1] + q[1])
            weights[at] = weights[at] + 0.5 * a * shifted(b, p)
    noise = noise.reshape(-1, NLON)
    rows = [scale * weights[r] * shifted(noise, r) for r in REACH]
    zero = jnp.zeros_like(noise)
    return jnp.stack(rows + [noise, zero, zero], axis=1)


def stencil(centre, east, west, north, south, c):
    return (c[0] * centre + (c[1] * east + c[2] * west)) + (c[3] * north + c[4] * south)


LINE = NLON + 16
GROUPS = 4


def wrap(ref, lines, tiles):
    for l in lines:
        for t in range(tiles):
            ref[t, l * LINE:l * LINE + 8, :] = ref[t, l * LINE + NLON:l * LINE + NLON + 8, :]
            ref[t, l * LINE + NLON + 8:(l + 1) * LINE, :] = ref[t, l * LINE + 8:l * LINE + 16, :]


def stage(source, target, added, coef, cycle, first, last, tiles, write=None):
    def group(i, carry):
        at = pl.multiple_of(i * (8 * GROUPS), 8 * GROUPS)
        for k in range(0, 8 * GROUPS, 8):
            def read(t, l, o=0):
                return source[t, pl.ds(at + (l * LINE + 8 + k + o), 8), :]

            south = [read(t, first - 1) for t in range(tiles)]
            centre = [read(t, first) for t in range(tiles)]
            for l in range(first, last):
                c = [coef[cycle * 5 + n, pl.ds(at + (l * NLON + k), 8), :] for n in range(5)]
                for t in range(tiles):
                    north = read(t, l + 1)
                    value = stencil(centre[t], read(t, l, 1), read(t, l, -1), north, south[t], c)
                    if added is not None:
                        value = value + added[t, pl.ds(at + (l * LINE + 8 + k), 8), :]
                    if write is None:
                        target[t, pl.ds(at + (l * LINE + 8 + k), 8), :] = value
                    else:
                        write(t, l, at + k, value)
                    south[t], centre[t] = centre[t], north
        return carry

    lax.fori_loop(0, NLON // (8 * GROUPS), group, 0)
    if write is None:
        wrap(target, range(first, last), tiles)


def fill_factors(compact_ref, factors):
    rows = compact_ref.shape[0]

    def body(i, carry):
        at = pl.ds(pl.multiple_of(i * 32, 32), 32)
        block = compact_ref[at, :]
        for n in range(5 * CYCLES):
            factors[n, at, :] = jnp.broadcast_to(block[:, n:n + 1], (32, 128))
        return carry

    lax.fori_loop(0, rows // 32, body, 0)


def row_kernel(lines, before_ref, mid_ref, after_ref, compact_ref, out_ref, factors, field, one, two):
    total = lines + 2 * HALO
    tiles = field.shape[0]

    @pl.when(pl.program_id(0) == 0)
    def _():
        fill_factors(compact_ref, factors)

    def copy(ref, first, count):
        for l in range(count):
            for t in range(tiles):
                field[t, (first + l) * LINE + 8:(first + l) * LINE + 8 + NLON, :] = ref[
                    l * NLON:(l + 1) * NLON, t * 128:(t + 1) * 128
                ]

    copy(before_ref, 0, HALO)
    copy(mid_ref, HALO, lines)
    copy(after_ref, HALO + lines, HALO)
    wrap(field, range(total), tiles)

    def write(t, l, at, value):
        out_ref[pl.ds(at + (l - HALO) * NLON, 8), t * 128:(t + 1) * 128] = value

    stage(field, one, None, factors, 0, 1, total - 1, tiles)
    stage(one, two, field, factors, 0, 2, total - 2, tiles)
    stage(two, field, None, factors, 1, 3, total - 3, tiles)
    stage(field, None, two, factors, 1, 4, total - 4, tiles, write)


def row_sections(before, block, after, compact, rows, columns, start):
    tile = 256
    lines, per = rows // NLON, columns // tile
    total = lines + 2 * HALO
    return pl.pallas_call(
        lambda *refs: row_kernel(lines, *refs),
        out_shape=jax.ShapeDtypeStruct((rows, columns), jnp.float32),
        grid=(per,),
        in_specs=[
            pl.BlockSpec((HALO * NLON, tile), lambda i: (0, i)),
            pl.BlockSpec((rows, tile), lambda i: (0, start // tile + i)),
            pl.BlockSpec((HALO * NLON, tile), lambda i: (0, i)),
            pl.BlockSpec(compact.shape, lambda i: (0, 0), pipeline_mode=pl.Buffered(1)),
        ],
        out_specs=pl.BlockSpec((rows, tile), lambda i: (0, i)),
        scratch_shapes=[pltpu.VMEM((5 * CYCLES, total * NLON, 128), jnp.float32)]
        + [pltpu.VMEM((tile // 128, total * LINE, 128), jnp.float32)] * 3,
        compiler_params=pltpu.CompilerParams(vmem_limit_bytes=48 << 20),
        cost_estimate=pl.CostEstimate(
            flops=60 * rows * columns, transcendentals=0, bytes_accessed=12 * rows * columns
        ),
        name="row_sections",
    )(before, block, after, compact)


def col_kernel(lines, widths, place_ref, *refs):
    pieces = refs[:len(widths)]
    compact_ref, noise_ref, out_ref, factors, field, one, two = refs[len(widths):]
    total = lines + 2 * HALO
    tiles = field.shape[0]

    @pl.when(pl.program_id(0) == 0)
    def _():
        fill_factors(compact_ref, factors)

    l = 0
    for ref, width in zip(pieces, widths):
        for k in range(width // NLON):
            for t in range(tiles):
                field[t, l * LINE + 8:l * LINE + 8 + NLON, :] = ref[
                    t * 128:(t + 1) * 128, k * NLON:(k + 1) * NLON
                ].T
            l += 1
    wrap(field, range(total), tiles)

    row = lax.broadcasted_iota(jnp.int32, (NLON, NLON), 0)
    lane = lax.broadcasted_iota(jnp.int32, (NLON, NLON), 1)
    apart = (row - lane + NLON) % NLON

    stage(field, one, None, factors, 0, 1, total - 1, tiles)
    stage(one, two, field, factors, 0, 2, total - 2, tiles)
    for t in range(tiles):
        shift = place_ref[0] + pl.program_id(0) * tiles + t - place_ref[1]
        for d in range(-2, 3):
            at = shift + (d + HALO)

            @pl.when((at >= 2) & (at < total - 2))
            def _():
                value = jnp.zeros((NLON, NLON), jnp.float32)
                for n, (dl, di) in enumerate(REACH):
                    if dl == d:
                        band = jnp.broadcast_to(noise_ref[t, n:n + 1, :], (NLON, NLON))
                        value = jnp.where(apart == di % NLON, band, value)
                rows = pl.ds(pl.multiple_of(at * LINE + 8, 8), NLON)
                two[t, rows, :] = two[t, rows, :] + value
                low = pl.ds(pl.multiple_of(at * LINE, 8), 8)
                two[t, low, :] = two[t, low, :] + value[NLON - 8:]
                high = pl.ds(pl.multiple_of(at * LINE + NLON + 8, 8), 8)
                two[t, high, :] = two[t, high, :] + value[:8]

    stage(two, field, None, factors, 1, 3, total - 3, tiles)
    stage(field, one, two, factors, 1, 4, total - 4, tiles)
    for t in range(tiles):
        shift = place_ref[0] + pl.program_id(0) * tiles + t - place_ref[1]

        for l in range(HALO, total - HALO):
            out_ref[t * 128:(t + 1) * 128, (l - HALO) * NLON:(l - HALO + 1) * NLON] = (
                0.0625 * one[t, l * LINE + 8:l * LINE + 8 + NLON, :]
            ).T

        @pl.when((shift >= 0) & (shift < lines))
        def _():
            cols = pl.ds(pl.multiple_of(shift * NLON, NLON), NLON)
            band = jnp.broadcast_to(noise_ref[t, len(REACH):len(REACH) + 1, :], (NLON, NLON))
            here = out_ref[t * 128:(t + 1) * 128, cols]
            out_ref[t * 128:(t + 1) * 128, cols] = here + jnp.where(apart == 0, band, 0.0)


def col_sections(place, pieces, compact, noise, rows, columns):
    widths = [p.shape[1] for p in pieces]
    tile = 256
    tiles = tile // NLON
    lines = columns // NLON
    total = lines + 2 * HALO
    return pl.pallas_call(
        lambda *refs: col_kernel(lines, widths, *refs),
        out_shape=jax.ShapeDtypeStruct((rows, columns), jnp.float32),
        grid_spec=pltpu.PrefetchScalarGridSpec(
            num_scalar_prefetch=1,
            grid=(rows // tile,),
            in_specs=[pl.BlockSpec((tile, w), lambda i, s: (i, 0)) for w in widths]
            + [
                pl.BlockSpec(compact.shape, lambda i, s: (0, 0), pipeline_mode=pl.Buffered(1)),
                pl.BlockSpec((tiles, 16, NLON), lambda i, s: (i, 0, 0)),
            ],
            out_specs=pl.BlockSpec((tile, columns), lambda i, s: (i, 0)),
            scratch_shapes=[pltpu.VMEM((5 * CYCLES, total * NLON, 128), jnp.float32)]
            + [pltpu.VMEM((tiles, total * LINE, 128), jnp.float32)] * 3,
        ),
        compiler_params=pltpu.CompilerParams(vmem_limit_bytes=56 << 20),
        cost_estimate=pl.CostEstimate(
            flops=60 * rows * columns, transcendentals=0, bytes_accessed=12 * rows * columns
        ),
        name="col_sections",
    )(place, *pieces, compact, noise)


def on_device(covariance, model_noise, east_wind, north_wind):
    rows, columns = covariance.shape
    row_lines, col_lines = rows // NLON, columns // NLON
    edge = HALO * NLON
    row_first = lax.axis_index("row") * row_lines
    col_first = lax.axis_index("col") * col_lines
    row_size, col_size = lax.axis_size("row"), lax.axis_size("col")
    row_up = [(i, i + 1) for i in range(row_size - 1)]
    row_down = [(j, i) for i, j in row_up]
    col_up = [(i, i + 1) for i in range(col_size - 1)]
    col_down = [(j, i) for i, j in col_up]

    half = edge // 2
    far = columns - edge
    order = [(0, half), (far, half), (half, half), (far + half, half)]
    order += [(c, edge) for c in range(edge, far, edge)]
    halos = {}
    for start, width in order:
        halos[start] = (
            lax.ppermute(covariance[rows - edge:, start:start + width], "row", row_up),
            lax.ppermute(covariance[:edge, start:start + width], "row", row_down),
        )

    coef = coefficients(east_wind, north_wind)

    def compact(first, lines):
        c = lines_of(coef, first, lines).reshape(5 * CYCLES, -1).T
        return jnp.pad(c, ((0, 0), (0, 16 - 5 * CYCLES)))

    row_coef = compact(row_first - HALO, row_lines + 2 * HALO)
    col_coef = compact(col_first - HALO, col_lines + 2 * HALO)
    noise = lax.dynamic_slice_in_dim(
        spread_noise(coef[1], model_noise, 8.0), row_first, row_lines, 0
    )

    mids, before, after = {}, [], []
    for start, width in order:
        mids[start] = row_sections(
            halos[start][0], covariance, halos[start][1], row_coef, rows, width, start
        )
        if start < edge:
            after.append(lax.ppermute(mids[start], "col", col_down))
        elif start >= far:
            before.append(lax.ppermute(mids[start], "col", col_up))
    place = jnp.stack([row_first, col_first]).astype(jnp.int32)
    pieces = before + [mids[start] for start in sorted(mids)] + after
    return col_sections(place, pieces, col_coef, noise, rows, columns)


def solution(mesh):
    in_specs = (P("row", "col"), P(), P(), P())
    out_specs = P("row", "col")
    return jax.shard_map(
        on_device, mesh=mesh, in_specs=in_specs, out_specs=out_specs, check_vma=False
    )
```

time: 646 us -> 221 us (0.34); the launches traced: 637 us -> 219 us
  other arithmetic: 367 us -> 5.43 us
  local copies, waits for them, and re-layouts: 185 us -> 43.7 us
  Pallas kernels: 0 us -> 117 us
  waiting for transfers between devices: 35.7 us -> 5.9 us
    add x26 -> x0, other arithmetic: 202 us -> none  [the longest x4 81.1 us: heun_section(): field + tendency(shaped(spread(matrix), lat_axis), east_here, faces_here,...]
    pallas_call x0 -> x7, Pallas kernels: none -> 117 us  [the longest x6 77.8 us: row_sections(): pl.pallas_call(lambda *refs: row_kernel(lines, *refs), out_shape=jax.Shap...]
    mul x4 -> x5, other arithmetic: 88.7 us -> 4.47 us  [spread_noise(): rows = [scale * weights[r] * shifted(noise, r) for r in REACH]]
    concatenate x8 -> x0, other arithmetic: 75.9 us -> none  [extended_2(): array = jnp.concatenate([before, array, after], axis=dim)]
    slice x32 -> x11, local copies, waits for them, and re-layouts: 68.3 us -> 14.5 us  [the longest x2 8.47 us: on_device(): covariance[:edge, start:start + width]]
    unnamed x67 -> x112, local copies, waits for them, and re-layouts: 51.8 us -> 7.3 us
    reshape x5 -> x2, local copies, waits for them, and re-layouts: 46.3 us -> 3.89 us  [compact(): c = lines_of(coef, first, lines).reshape(5 * CYCLES, -1).T]
    ppermute x16, waiting for transfers between devices: 35.7 us -> 5.9 us  [the longest x2 5.86 us: on_device(): after.append(lax.ppermute(mids[start], 'col', col_down))]
  transfers between devices with their start and end apart: 16 -> 16, of which waited for: 7 -> 1; matrix products, arithmetic and copies ran while one was open for 15% -> 17% of each run, Pallas kernels for 0% -> 35%
where the time goes in v2:
time: 221 us; the launch traced here: 219 us
  Pallas kernels  117 us (53%)
  starting transfers between devices  46.8 us (21%)
  local copies, waits for them, and re-layouts  43.7 us (20%)
  waiting for transfers between devices  5.9 us (3%)
  other arithmetic  5.43 us (2%)
    pallas_call x6, Pallas kernels, row_sections(): pl.pallas_call(lambda *refs: row_kernel(lines, *refs), out_shape=jax.Shap...  77.8 us
    pallas_call x1, Pallas kernels, col_sections(): pl.pallas_call(lambda *refs: col_kernel(lines, widths, *refs), out_shape=...  39 us
    ppermute x6, starting transfers between devices, on_device(): lax.ppermute(covariance[rows - edge:, start:start + width], 'row', row_up)  22.2 us
    ppermute x6, starting transfers between devices, on_device(): lax.ppermute(covariance[:edge, start:start + width], 'row', row_down)  13.8 us
    slice x2, local copies, waits for them, and re-layouts, on_device(): covariance[:edge, start:start + width]  8.47 us
    ppermute x2, starting transfers between devices, on_device(): before.append(lax.ppermute(mids[start], 'col', col_up))  7.96 us
    unnamed x112, local copies, waits for them, and re-layouts  7.3 us
    ppermute x2, waiting for transfers between devices, on_device(): after.append(lax.ppermute(mids[start], 'col', col_down))  5.86 us
  transfers between devices with their start and end apart: 16, of which 1 were waited for; matrix products, arithmetic and copies ran while one was open for 17% of the time, Pallas kernels for 35%

profile of v2, /device:TPU:2, one launch (start us, length us, event | category | flops | bytes accessed | tf_op | source)
XLA Modules:
  0.0 219.4 jit_solution(15855328650549008052)
XLA Ops:
  0.0 4.3 %fusion.42 = (f32[512,256]{1,0:T(8,128)}, f32[512,256]{1,0:T(8,128)}, f32[512,256]{1,0:T(8,128)}, f32[512,256]{1,0:T(8,128)}, f32[512,256]{1,0:T(8,128)}, /*inde...) fusion(f32[1024,2048]{1,0:T(8,128)} %refs_1_.11), kind=kLoop, calls=%fused_computation.121 | loop fusion | bytes 8388608 | tf_op jit(solution)/shard_map/slice | solution.py:280
  4.3 1.9 collective-permute-start.9
  6.2 2.4 %collective-permute-start.8 = (f32[512,256]{1,0:T(8,128)}, f32[512,256]{1,0:T(8,128)S(1)}, u32[]{:S(2)}, u32[]{:S(2)}) collective-permute-start(f32[512,256]{1,0:T(8,128)} %get-tuple-element.16), channel_id=1, source_target_pairs={{0,4},{4,8},{8,12},{12,16},{16,20},{20,24},{24,28},{1,5},{5,9},{9,... | collective-permute-start | bytes 1572872 | tf_op jit(solution)/shard_map/ppermute | solution.py:279
  8.6 3.2 %collective-permute-start.7 = (f32[512,256]{1,0:T(8,128)}, f32[512,256]{1,0:T(8,128)S(1)}, u32[]{:S(2)}, u32[]{:S(2)}) collective-permute-start(f32[512,256]{1,0:T(8,128)} %get-tuple-element.17), channel_id=1, source_target_pairs={{4,0},{8,4},{12,8},{16,12},{20,16},{24,20},{28,24},{5,1},{9,5},{13... | collective-permute-start | bytes 1572872 | tf_op jit(solution)/shard_map/ppermute | solution.py:280
  11.8 2.6 %collective-permute-start.6 = (f32[512,256]{1,0:T(8,128)}, f32[512,256]{1,0:T(8,128)S(1)}, u32[]{:S(2)}, u32[]{:S(2)}) collective-permute-start(f32[512,256]{1,0:T(8,128)} %get-tuple-element.18), channel_id=1, source_target_pairs={{0,4},{4,8},{8,12},{12,16},{16,20},{20,24},{24,28},{1,5},{5,9},{9,... | collective-permute-start | bytes 1572872 | tf_op jit(solution)/shard_map/ppermute | solution.py:279
  14.4 2.9 %collective-permute-start.1 = (f32[512,256]{1,0:T(8,128)}, f32[512,256]{1,0:T(8,128)S(1)}, u32[]{:S(2)}, u32[]{:S(2)}) collective-permute-start(f32[512,256]{1,0:T(8,128)} %get-tuple-element.21), channel_id=1, source_target_pairs={{4,0},{8,4},{12,8},{16,12},{20,16},{24,20},{28,24},{5,1},{9,5},{13... | collective-permute-start | bytes 1572872 | tf_op jit(solution)/shard_map/ppermute | solution.py:280
  27.4 4.2 %fusion.41 = (f32[512,512]{1,0:T(8,128)}, f32[512,512]{1,0:T(8,128)}, f32[512,512]{1,0:T(8,128)}, f32[512,512]{1,0:T(8,128)}) fusion(f32[1024,2048]{1,0:T(8,128)} %refs_1_.11), kind=kLoop, calls=%fused_computation.120 | loop fusion | bytes 8388608 | tf_op jit(solution)/shard_map/slice | solution.py:280
  31.7 3.5 %collective-permute-start = (f32[512,256]{1,0:T(8,128)}, f32[512,256]{1,0:T(8,128)S(1)}, u32[]{:S(2)}, u32[]{:S(2)}) collective-permute-start(f32[512,256]{1,0:T(8,128)} %get-tuple-element.22), channel_id=1, source_target_pairs={{0,4},{4,8},{8,12},{12,16},{16,20},{20,24},{24,28},{1,5},{5,9},{9,... | collective-permute-start | bytes 1572872 | tf_op jit(solution)/shard_map/ppermute | solution.py:279
  35.3 2.0 collective-permute-start.13
  37.3 4.4 %collective-permute-start.12 = (f32[512,512]{1,0:T(8,128)}, f32[512,512]{1,0:T(8,128)}, u32[]{:S(2)}, u32[]{:S(2)}) collective-permute-start(f32[512,512]{1,0:T(8,128)} %get-tuple-element.12), channel_id=1, source_target_pairs={{0,4},{4,8},{8,12},{12,16},{16,20},{20,24},{24,28},{1,5},{5,9},{9,... | collective-permute-start | bytes 3145736 | tf_op jit(solution)/shard_map/ppermute | solution.py:279
  41.8 1.9 collective-permute-start.11
  47.0 2.2 %copy.34 = f32[10,2048]{0,1:T(8,128)} copy(f32[10,2048]{1,0:T(8,128)} %bitcast.204) | data formatting | bytes 163840 | tf_op jit(solution)/shard_map/reshape | solution.py:286
  50.6 1.7 copy.36
  52.2 2.7 %pad.70.refs_11_ = f32[3072,16]{1,0:T(8,128)} pad(f32[3072,10]{1,0:T(8,128)} %bitcast.197, f32[]{:T(128)} %constant.36.clone.1), padding=0_0x0_6 | pad | bytes 319492 | tf_op jit(solution)/shard_map/jit(_pad)/pad | solution.py:287
  56.7 1.9 collective-permute-start.4
  59.4 4.5 %collective-permute-start.3 = (f32[512,256]{1,0:T(8,128)}, f32[512,256]{1,0:T(8,128)S(1)}, u32[]{:S(2)}, u32[]{:S(2)}) collective-permute-start(f32[512,256]{1,0:T(8,128)} %get-tuple-element.20), channel_id=1, source_target_pairs={{0,4},{4,8},{8,12},{12,16},{16,20},{20,24},{24,28},{1,5},{5,9},{9,... | collective-permute-start | bytes 1572872 | tf_op jit(solution)/shard_map/ppermute | solution.py:279
  65.7 1.6 fusion.35
  67.3 11.5 %row_sections.9.refs_4_ = f32[1024,256]{1,0:T(8,128)S(1)} custom-call(f32[512,256]{1,0:T(8,128)S(1)} %collective-permute-done.8.refs_0_, f32[1024,2048]{1,0:T(8,128)} %refs_1_.11, f32[512,256]{1,0:T(8,128)S(1)} %collective-permute-done.9.refs_2_, f32[2048,16]{1,0:T(8,128)S(1)} %pad.69.refs_3_), custom_call_target="tpu_custom_call" | custom-call | flops 15728640 | bytes 3145728 | tf_op jit(solution)/shard_map/row_sections/pallas_call | solution.py:147
  80.9 11.9 %row_sections.8.refs_3_ = f32[1024,256]{1,0:T(8,128)S(1)} custom-call(f32[512,256]{1,0:T(8,128)S(1)} %copy-done.7, f32[1024,2048]{1,0:T(8,128)} %refs_1_.11, f32[512,256]{1,0:T(8,128)S(1)} %copy-done.5, f32[2048,16]{1,0:T(8,128)S(1)} %pad.69.refs_3_), custom_call_target="tpu_custom_call" | custom-call | flops 15728640 | bytes 3145728 | tf_op jit(solution)/shard_map/row_sections/pallas_call | solution.py:147
  92.8 12.8 %row_sections.6.refs_7_ = f32[1024,256]{1,0:T(8,128)} custom-call(f32[512,256]{1,0:T(8,128)S(1)} %copy-done.11, f32[1024,2048]{1,0:T(8,128)} %refs_1_.11, f32[512,256]{1,0:T(8,128)S(1)} %copy-done.9, f32[2048,16]{1,0:T(8,128)S(1)} %pad.69.refs_3_), custom_call_target="tpu_custom_call" | custom-call | flops 15728640 | bytes 3145728 | tf_op jit(solution)/shard_map/row_sections/pallas_call | solution.py:147
  105.9 4.7 %collective-permute-start.10 = (f32[512,512]{1,0:T(8,128)}, f32[512,512]{1,0:T(8,128)}, u32[]{:S(2)}, u32[]{:S(2)}) collective-permute-start(f32[512,512]{1,0:T(8,128)} %get-tuple-element.14), channel_id=1, source_target_pairs={{0,4},{4,8},{8,12},{12,16},{16,20},{20,24},{24,28},{1,5},{5,9},{9,... | collective-permute-start | bytes 3145736 | tf_op jit(solution)/shard_map/ppermute | solution.py:279
  110.6 4.5 %collective-permute-start.2 = (f32[1024,256]{1,0:T(8,128)}, f32[1024,256]{1,0:T(8,128)}, u32[]{:S(2)}, u32[]{:S(2)}) collective-permute-start(f32[1024,256]{1,0:T(8,128)} %row_sections.6.refs_7_), channel_id=1, source_target_pairs={{0,1},{1,2},{2,3},{4,5},{5,6},{6,7},{8,9},{9,10},{10,11},{12,13},{... | collective-permute-start | bytes 3145736 | tf_op jit(solution)/shard_map/ppermute | solution.py:303
  115.0 12.5 %row_sections.7.refs_8_ = f32[1024,256]{1,0:T(8,128)} custom-call(f32[512,256]{1,0:T(8,128)S(1)} %collective-permute-done.3.refs_0_, f32[1024,2048]{1,0:T(8,128)} %refs_1_.11, f32[512,256]{1,0:T(8,128)S(1)} %collective-permute-done.4.refs_2_, f32[2048,16]{1,0:T(8,128)S(1)} %pad.69.refs_3_), custom_call_target="tpu_custom_call" | custom-call | flops 15728640 | bytes 3145728 | tf_op jit(solution)/shard_map/row_sections/pallas_call | solution.py:147
  127.5 3.5 %collective-permute-start.5 = (f32[1024,256]{1,0:T(8,128)}, f32[1024,256]{1,0:T(8,128)}, u32[]{:S(2)}, u32[]{:S(2)}) collective-permute-start(f32[1024,256]{1,0:T(8,128)} %row_sections.7.refs_8_), channel_id=1, source_target_pairs={{0,1},{1,2},{2,3},{4,5},{5,6},{6,7},{8,9},{9,10},{10,11},{12,13},{... | collective-permute-start | bytes 3145736 | tf_op jit(solution)/shard_map/ppermute | solution.py:303
  132.3 1.5 collective-permute-start.15
  137.0 3.7 %stack.80 = f32[64,16,128]{2,1,0:T(8,128)} concatenate(f32[64,1,128]{2,1,0:T(1,128)} %bitcast.210, f32[64,1,128]{2,1,0:T(1,128)} %bitcast.209, f32[64,1,128]{2,1,0:T(1,128)} %bitcast.216, f32[64,1,128]{2,1,0:T(1,128)} %bitcast.217, f32[64,1,128]{2,1,0:T(1,128)} %bitcast.220, f32[64,1,128]{2,1,0:T(1,128)} %bitcast.213, f32[64,1,128]{2,1,0:T(1,128)} %bitcast.219, ...), dimensions={1} | concatenate | bytes 1048576 | tf_op jit(solution)/shard_map/stack | solution.py:55
  141.3 1.5 constant_dynamic-slice_fusion.refs_12_
  142.8 14.6 %row_sections.11.refs_6_ = f32[1024,512]{1,0:T(8,128)S(1)} custom-call(f32[512,512]{1,0:T(8,128)} %collective-permute-done.12.refs_0_, f32[1024,2048]{1,0:T(8,128)} %refs_1_.11, f32[512,512]{1,0:T(8,128)} %collective-permute-done.13.refs_2_, f32[2048,16]{1,0:T(8,128)S(1)} %pad.69.refs_3_), custom_call_target="tpu_custom_call" | custom-call | flops 31457280 | bytes 6291456 | tf_op jit(solution)/shard_map/row_sections/pallas_call | solution.py:147
  158.7 14.6 %row_sections.10.refs_5_ = f32[1024,512]{1,0:T(8,128)S(1)} custom-call(f32[512,512]{1,0:T(8,128)} %collective-permute-done.10.refs_0_, f32[1024,2048]{1,0:T(8,128)} %refs_1_.11, f32[512,512]{1,0:T(8,128)} %collective-permute-done.11.refs_2_, f32[2048,16]{1,0:T(8,128)S(1)} %pad.69.refs_3_), custom_call_target="tpu_custom_call" | custom-call | flops 31457280 | bytes 6291456 | tf_op jit(solution)/shard_map/row_sections/pallas_call | solution.py:147
  173.3 1.3 copy-done.1
  174.6 5.9 %collective-permute-done.15.refs_10_ = f32[1024,256]{1,0:T(8,128)} collective-permute-done((f32[1024,256]{1,0:T(8,128)S(1)}, f32[1024,256]{1,0:T(8,128)}, u32[]{:S(2)}, u32[]{:S(2)}) %collective-permute-start.15) | collective-permute-done | bytes 1048608 | tf_op jit(solution)/shard_map/ppermute | solution.py:301
  180.5 39.0 %col_sections.1 = f32[1024,2048]{1,0:T(8,128)} custom-call(s32[2]{0:T(128)} %pad_add_fusion.refs_0_, f32[1024,256]{1,0:T(8,128)} %collective-permute-done.2.refs_1_, f32[1024,256]{1,0:T(8,128)} %collective-permute-done.5.refs_2_, f32[1024,256]{1,0:T(8,128)} %copy-done.3, f32[1024,256]{1,0:T(8,128)} %copy-done.2, f32[1024,512]{1,0:T(8,128)} %copy-done.1, ...), custom_call_target="tpu_custom_call" | custom-call | flops 125829120 | bytes 25165824 | tf_op jit(solution)/shard_map/col_sections/pallas_call | solution.py:237
  (168 shorter events, 27.3 us)
Async XLA Ops:
  4.3 27.4 %collective-permute-start.9 = (f32[512,256]{1,0:T(8,128)}, f32[512,256]{1,0:T(8,128)S(1)}, u32[]{:S(2)}, u32[]{:S(2)}) collective-permute-start(f32[512,256]{1,0:T(8,128)} %get-tuple-element.15), channel_id=1, source_target_pairs={{4,0},{8,4},{12,8},{16,12},{20,16},{24,20},{28,24},{5,1},{9,5},{13... | collective-permute-start | bytes 1572872 | tf_op jit(solution)/shard_map/ppermute | solution.py:280
  6.2 29.1 %collective-permute-start.8 = (f32[512,256]{1,0:T(8,128)}, f32[512,256]{1,0:T(8,128)S(1)}, u32[]{:S(2)}, u32[]{:S(2)}) collective-permute-start(f32[512,256]{1,0:T(8,128)} %get-tuple-element.16), channel_id=1, source_target_pairs={{0,4},{4,8},{8,12},{12,16},{16,20},{20,24},{24,28},{1,5},{5,9},{9,... | collective-permute-start | bytes 1572872 | tf_op jit(solution)/shard_map/ppermute | solution.py:279
  8.6 28.7 %collective-permute-start.7 = (f32[512,256]{1,0:T(8,128)}, f32[512,256]{1,0:T(8,128)S(1)}, u32[]{:S(2)}, u32[]{:S(2)}) collective-permute-start(f32[512,256]{1,0:T(8,128)} %get-tuple-element.17), channel_id=1, source_target_pairs={{4,0},{8,4},{12,8},{16,12},{20,16},{24,20},{28,24},{5,1},{9,5},{13... | collective-permute-start | bytes 1572872 | tf_op jit(solution)/shard_map/ppermute | solution.py:280
  11.8 30.0 %collective-permute-start.6 = (f32[512,256]{1,0:T(8,128)}, f32[512,256]{1,0:T(8,128)S(1)}, u32[]{:S(2)}, u32[]{:S(2)}) collective-permute-start(f32[512,256]{1,0:T(8,128)} %get-tuple-element.18), channel_id=1, source_target_pairs={{0,4},{4,8},{8,12},{12,16},{16,20},{20,24},{24,28},{1,5},{5,9},{9,... | collective-permute-start | bytes 1572872 | tf_op jit(solution)/shard_map/ppermute | solution.py:279
  14.4 41.4 %collective-permute-start.1 = (f32[512,256]{1,0:T(8,128)}, f32[512,256]{1,0:T(8,128)S(1)}, u32[]{:S(2)}, u32[]{:S(2)}) collective-permute-start(f32[512,256]{1,0:T(8,128)} %get-tuple-element.21), channel_id=1, source_target_pairs={{4,0},{8,4},{12,8},{16,12},{20,16},{24,20},{28,24},{5,1},{9,5},{13... | collective-permute-start | bytes 1572872 | tf_op jit(solution)/shard_map/ppermute | solution.py:280
  31.7 26.9 %collective-permute-start = (f32[512,256]{1,0:T(8,128)}, f32[512,256]{1,0:T(8,128)S(1)}, u32[]{:S(2)}, u32[]{:S(2)}) collective-permute-start(f32[512,256]{1,0:T(8,128)} %get-tuple-element.22), channel_id=1, source_target_pairs={{0,4},{4,8},{8,12},{12,16},{16,20},{20,24},{24,28},{1,5},{5,9},{9,... | collective-permute-start | bytes 1572872 | tf_op jit(solution)/shard_map/ppermute | solution.py:279
  35.3 92.2 %collective-permute-start.13 = (f32[512,512]{1,0:T(8,128)}, f32[512,512]{1,0:T(8,128)}, u32[]{:S(2)}, u32[]{:S(2)}) collective-permute-start(f32[512,512]{1,0:T(8,128)} %get-tuple-element.11), channel_id=1, source_target_pairs={{4,0},{8,4},{12,8},{16,12},{20,16},{24,20},{28,24},{5,1},{9,5},{13... | collective-permute-start | bytes 3145736 | tf_op jit(solution)/shard_map/ppermute | solution.py:280
  37.3 93.7 %collective-permute-start.12 = (f32[512,512]{1,0:T(8,128)}, f32[512,512]{1,0:T(8,128)}, u32[]{:S(2)}, u32[]{:S(2)}) collective-permute-start(f32[512,512]{1,0:T(8,128)} %get-tuple-element.12), channel_id=1, source_target_pairs={{0,4},{4,8},{8,12},{12,16},{16,20},{20,24},{24,28},{1,5},{5,9},{9,... | collective-permute-start | bytes 3145736 | tf_op jit(solution)/shard_map/ppermute | solution.py:279
  41.8 90.5 %collective-permute-start.11 = (f32[512,512]{1,0:T(8,128)}, f32[512,512]{1,0:T(8,128)}, u32[]{:S(2)}, u32[]{:S(2)}) collective-permute-start(f32[512,512]{1,0:T(8,128)} %get-tuple-element.13), channel_id=1, source_target_pairs={{4,0},{8,4},{12,8},{16,12},{20,16},{24,20},{28,24},{5,1},{9,5},{13... | collective-permute-start | bytes 3145736 | tf_op jit(solution)/shard_map/ppermute | solution.py:280
  56.7 49.2 %collective-permute-start.4 = (f32[512,256]{1,0:T(8,128)}, f32[512,256]{1,0:T(8,128)S(1)}, u32[]{:S(2)}, u32[]{:S(2)}) collective-permute-start(f32[512,256]{1,0:T(8,128)} %get-tuple-element.19), channel_id=1, source_target_pairs={{4,0},{8,4},{12,8},{16,12},{20,16},{24,20},{28,24},{5,1},{9,5},{13... | collective-permute-start | bytes 1572872 | tf_op jit(solution)/shard_map/ppermute | solution.py:280
  59.4 51.2 %collective-permute-start.3 = (f32[512,256]{1,0:T(8,128)}, f32[512,256]{1,0:T(8,128)S(1)}, u32[]{:S(2)}, u32[]{:S(2)}) collective-permute-start(f32[512,256]{1,0:T(8,128)} %get-tuple-element.20), channel_id=1, source_target_pairs={{0,4},{4,8},{8,12},{12,16},{16,20},{20,24},{24,28},{1,5},{5,9},{9,... | collective-permute-start | bytes 1572872 | tf_op jit(solution)/shard_map/ppermute | solution.py:279
  80.9 51.5 %copy-start.2 = (f32[1024,256]{1,0:T(8,128)}, f32[1024,256]{1,0:T(8,128)S(1)}, u32[]{:S(2)}) copy-start(f32[1024,256]{1,0:T(8,128)S(1)} %row_sections.9.refs_4_) | copy-start | bytes 3145732
  92.8 38.3 %copy-start.3 = (f32[1024,256]{1,0:T(8,128)}, f32[1024,256]{1,0:T(8,128)S(1)}, u32[]{:S(2)}) copy-start(f32[1024,256]{1,0:T(8,128)S(1)} %row_sections.8.refs_3_) | copy-start | bytes 3145732
  105.7 29.7 %copy-start.24 = (f32[2,64,128]{2,1,0:T(8,128)S(1)}, f32[2,64,128]{2,1,0:T(8,128)}, u32[]{:S(2)}) copy-start(f32[2,64,128]{2,1,0:T(8,128)} %copy-done.23) | copy-start | bytes 196612
  105.7 29.7 %copy-start.26 = (f32[63,128]{1,0:T(8,128)S(1)}, f32[63,128]{1,0:T(8,128)}, u32[]{:S(2)}) copy-start(f32[63,128]{1,0:T(8,128)} %copy-done.25) | copy-start | bytes 96772
  105.7 29.7 %copy-start.28 = (f32[63,128]{1,0:T(8,128)S(1)}, f32[63,128]{1,0:T(8,128)}, u32[]{:S(2)}) copy-start(f32[63,128]{1,0:T(8,128)} %copy-done.27) | copy-start | bytes 96772
  105.7 29.7 %copy-start.29 = (f32[62,128]{1,0:T(8,128)S(1)}, f32[62,128]{1,0:T(8,128)}, u32[]{:S(2)}) copy-start(f32[62,128]{1,0:T(8,128)} %get-tuple-element.49) | copy-start | bytes 95236
  105.7 29.7 %copy-start.32 = (f32[63,128]{1,0:T(8,128)S(1)}, f32[63,128]{1,0:T(8,128)}, u32[]{:S(2)}) copy-start(f32[63,128]{1,0:T(8,128)} %get-tuple-element.61) | copy-start | bytes 96772
  105.7 29.7 %copy-start.33 = (f32[63,128]{1,0:T(8,128)S(1)}, f32[63,128]{1,0:T(8,128)}, u32[]{:S(2)}) copy-start(f32[63,128]{1,0:T(8,128)} %get-tuple-element.62) | copy-start | bytes 96772
  105.7 29.7 %copy-start.35 = (f32[64,127]{1,0:T(8,128)S(1)}, f32[64,127]{1,0:T(8,128)}, u32[]{:S(2)}) copy-start(f32[64,127]{1,0:T(8,128)} %get-tuple-element.98) | copy-start | bytes 97540
  105.8 30.4 %copy-start.34 = (f32[64,127]{1,0:T(8,128)S(1)}, f32[64,127]{1,0:T(8,128)}, u32[]{:S(2)}) copy-start(f32[64,127]{1,0:T(8,128)} %get-tuple-element.53) | copy-start | bytes 97540
  105.8 30.4 %copy-start.36 = (f32[64,1]{1,0:T(8,128)S(1)}, f32[64,1]{1,0:T(8,128)}, u32[]{:S(2)}) copy-start(f32[64,1]{1,0:T(8,128)} %get-tuple-element.59) | copy-start | bytes 772
  105.8 30.4 %copy-start.37 = (f32[64,127]{1,0:T(8,128)S(1)}, f32[64,127]{1,0:T(8,128)}, u32[]{:S(2)}) copy-start(f32[64,127]{1,0:T(8,128)} %get-tuple-element.57) | copy-start | bytes 97540
  105.8 30.4 %copy-start.40 = (f32[64,127]{1,0:T(8,128)S(1)}, f32[64,127]{1,0:T(8,128)}, u32[]{:S(2)}) copy-start(f32[64,127]{1,0:T(8,128)} %get-tuple-element.70) | copy-start | bytes 97540
  105.8 30.4 %copy-start.41 = (f32[64,127]{1,0:T(8,128)S(1)}, f32[64,127]{1,0:T(8,128)}, u32[]{:S(2)}) copy-start(f32[64,127]{1,0:T(8,128)} %get-tuple-element.114) | copy-start | bytes 97540
  105.8 30.4 %copy-start.42 = (f32[64,1]{1,0:T(8,128)S(1)}, f32[64,1]{1,0:T(8,128)}, u32[]{:S(2)}) copy-start(f32[64,1]{1,0:T(8,128)} %get-tuple-element.72) | copy-start | bytes 772
  105.8 30.4 %copy-start.43 = (f32[64,1]{1,0:T(8,128)S(1)}, f32[64,1]{1,0:T(8,128)}, u32[]{:S(2)}) copy-start(f32[64,1]{1,0:T(8,128)} %get-tuple-element.112) | copy-start | bytes 772
  105.9 52.8 %collective-permute-start.10 = (f32[512,512]{1,0:T(8,128)}, f32[512,512]{1,0:T(8,128)}, u32[]{:S(2)}, u32[]{:S(2)}) collective-permute-start(f32[512,512]{1,0:T(8,128)} %get-tuple-element.14), channel_id=1, source_target_pairs={{0,4},{4,8},{8,12},{12,16},{16,20},{20,24},{24,28},{1,5},{5,9},{9,... | collective-permute-start | bytes 3145736 | tf_op jit(solution)/shard_map/ppermute | solution.py:279
  110.6 64.1 %collective-permute-start.2 = (f32[1024,256]{1,0:T(8,128)}, f32[1024,256]{1,0:T(8,128)}, u32[]{:S(2)}, u32[]{:S(2)}) collective-permute-start(f32[1024,256]{1,0:T(8,128)} %row_sections.6.refs_7_), channel_id=1, source_target_pairs={{0,1},{1,2},{2,3},{4,5},{5,6},{6,7},{8,9},{9,10},{10,11},{12,13},{... | collective-permute-start | bytes 3145736 | tf_op jit(solution)/shard_map/ppermute | solution.py:303
  127.5 47.1 %collective-permute-start.5 = (f32[1024,256]{1,0:T(8,128)}, f32[1024,256]{1,0:T(8,128)}, u32[]{:S(2)}, u32[]{:S(2)}) collective-permute-start(f32[1024,256]{1,0:T(8,128)} %row_sections.7.refs_8_), channel_id=1, source_target_pairs={{0,1},{1,2},{2,3},{4,5},{5,6},{6,7},{8,9},{9,10},{10,11},{12,13},{... | collective-permute-start | bytes 3145736 | tf_op jit(solution)/shard_map/ppermute | solution.py:303
  131.0 43.6 %collective-permute-start.14 = (f32[1024,256]{1,0:T(8,128)S(1)}, f32[1024,256]{1,0:T(8,128)}, u32[]{:S(2)}, u32[]{:S(2)}) collective-permute-start(f32[1024,256]{1,0:T(8,128)S(1)} %row_sections.8.refs_3_), channel_id=1, source_target_pairs={{1,0},{2,1},{3,2},{5,4},{6,5},{7,6},{9,8},{10,9},{11,10},{13,12},{... | collective-permute-start | bytes 3145736 | tf_op jit(solution)/shard_map/ppermute | solution.py:301
  132.3 48.2 %collective-permute-start.15 = (f32[1024,256]{1,0:T(8,128)S(1)}, f32[1024,256]{1,0:T(8,128)}, u32[]{:S(2)}, u32[]{:S(2)}) collective-permute-start(f32[1024,256]{1,0:T(8,128)S(1)} %row_sections.9.refs_4_), channel_id=1, source_target_pairs={{1,0},{2,1},{3,2},{5,4},{6,5},{7,6},{9,8},{10,9},{11,10},{13,12},{... | collective-permute-start | bytes 3145736 | tf_op jit(solution)/shard_map/ppermute | solution.py:301
  (38 other events, 672.2 us)

commit v3 on v2

--- a/solution.py
+++ b/solution.py
@@ -111,13 +111,9 @@
     lax.fori_loop(0, rows // 32, body, 0)
 
 
-def row_kernel(lines, before_ref, mid_ref, after_ref, compact_ref, out_ref, factors, field, one, two):
+def row_kernel(lines, before_ref, mid_ref, after_ref, factors, out_ref, field, one, two):
     total = lines + 2 * HALO
     tiles = field.shape[0]
-
-    @pl.when(pl.program_id(0) == 0)
-    def _():
-        fill_factors(compact_ref, factors)
 
     def copy(ref, first, count):
         for l in range(count):
@@ -140,7 +136,7 @@
     stage(field, None, two, factors, 1, 4, total - 4, tiles, write)
 
 
-def row_sections(before, block, after, compact, rows, columns, start):
+def row_sections(before, block, after, factors, rows, columns, start):
     tile = 256
     lines, per = rows // NLON, columns // tile
     total = lines + 2 * HALO
@@ -152,17 +148,16 @@
             pl.BlockSpec((HALO * NLON, tile), lambda i: (0, i)),
             pl.BlockSpec((rows, tile), lambda i: (0, start // tile + i)),
             pl.BlockSpec((HALO * NLON, tile), lambda i: (0, i)),
-            pl.BlockSpec(compact.shape, lambda i: (0, 0), pipeline_mode=pl.Buffered(1)),
+            pl.BlockSpec(factors.shape, lambda i: (0, 0, 0), pipeline_mode=pl.Buffered(1)),
         ],
         out_specs=pl.BlockSpec((rows, tile), lambda i: (0, i)),
-        scratch_shapes=[pltpu.VMEM((5 * CYCLES, total * NLON, 128), jnp.float32)]
-        + [pltpu.VMEM((tile // 128, total * LINE, 128), jnp.float32)] * 3,
+        scratch_shapes=[pltpu.VMEM((tile // 128, total * LINE, 128), jnp.float32)] * 3,
         compiler_params=pltpu.CompilerParams(vmem_limit_bytes=48 << 20),
         cost_estimate=pl.CostEstimate(
             flops=60 * rows * columns, transcendentals=0, bytes_accessed=12 * rows * columns
         ),
         name="row_sections",
-    )(before, block, after, compact)
+    )(before, block, after, factors)
 
 
 def col_kernel(lines, widths, place_ref, *refs):
@@ -269,10 +264,8 @@
     col_up = [(i, i + 1) for i in range(col_size - 1)]
     col_down = [(j, i) for i, j in col_up]
 
-    half = edge // 2
     far = columns - edge
-    order = [(0, half), (far, half), (half, half), (far + half, half)]
-    order += [(c, edge) for c in range(edge, far, edge)]
+    order = [(0, edge), (far, edge)] + ([(edge, far - edge)] if far > edge else [])
     halos = {}
     for start, width in order:
         halos[start] = (
@@ -286,7 +279,8 @@
         c = lines_of(coef, first, lines).reshape(5 * CYCLES, -1).T
         return jnp.pad(c, ((0, 0), (0, 16 - 5 * CYCLES)))
 
-    row_coef = compact(row_first - HALO, row_lines + 2 * HALO)
+    row_coef = lines_of(coef, row_first - HALO, row_lines + 2 * HALO).reshape(5 * CYCLES, -1)
+    row_coef = jnp.broadcast_to(row_coef[:, :, None], row_coef.shape + (128,))
     col_coef = compact(col_first - HALO, col_lines + 2 * HALO)
     noise = lax.dynamic_slice_in_dim(
         spread_noise(coef[1], model_noise, 8.0), row_first, row_lines, 0

time: 221 us -> 179 us (0.81)
  Pallas kernels: 117 us -> 75.3 us
  waiting for transfers between devices: 5.9 us -> 32.1 us
  starting transfers between devices: 46.8 us -> 25.6 us
  local copies, waits for them, and re-layouts: 43.7 us -> 36.9 us
    pallas_call x6 -> x3, Pallas kernels: 77.8 us -> 36.3 us  [row_sections(): pl.pallas_call(lambda *refs: row_kernel(lines, *refs), out_shape=jax.Shap...]
    ppermute x6 -> x3, starting transfers between devices: 22.2 us -> 11.3 us  [on_device(): lax.ppermute(covariance[rows - edge:, start:start + width], 'row', row_up)]
    ppermute x2 -> x1, waiting for transfers between devices: 5.86 us -> 16.3 us  [on_device(): after.append(lax.ppermute(mids[start], 'col', col_down))]
    ppermute x6 -> x3, waiting for transfers between devices: 0.02 us -> 10 us  [on_device(): lax.ppermute(covariance[:edge, start:start + width], 'row', row_down)]
    broadcast_in_dim x0 -> x1, local copies, waits for them, and re-layouts: none -> 6.85 us  [on_device(): row_coef = jnp.broadcast_to(row_coef[:, :, None], row_coef.shape + (128,))]
    ppermute x6 -> x3, starting transfers between devices: 13.8 us -> 8.11 us  [on_device(): lax.ppermute(covariance[:edge, start:start + width], 'row', row_down)]
    ppermute x2 -> x1, waiting for transfers between devices: 0.01 us -> 5.68 us  [on_device(): before.append(lax.ppermute(mids[start], 'col', col_up))]
    unnamed x112 -> x86, local copies, waits for them, and re-layouts: 7.3 us -> 2.88 us
  transfers between devices with their start and end apart: 16 -> 8, of which waited for: 1 -> 3; matrix products, arithmetic and copies ran while one was open for 17% -> 21% of each run, Pallas kernels for 35% -> 20%
where the time goes in v3:
time: 179 us; the launch traced here: 178 us
  Pallas kernels  75.3 us (42%)
  local copies, waits for them, and re-layouts  36.9 us (21%)
  waiting for transfers between devices  32.1 us (18%)
  starting transfers between devices  25.6 us (14%)
  other arithmetic  7.53 us (4%)
    pallas_call x1, Pallas kernels, col_sections(): pl.pallas_call(lambda *refs: col_kernel(lines, widths, *refs), out_shape=...  38.9 us
    pallas_call x3, Pallas kernels, row_sections(): pl.pallas_call(lambda *refs: row_kernel(lines, *refs), out_shape=jax.Shap...  36.3 us
    ppermute x1, waiting for transfers between devices, on_device(): after.append(lax.ppermute(mids[start], 'col', col_down))  16.3 us
    ppermute x3, starting transfers between devices, on_device(): lax.ppermute(covariance[rows - edge:, start:start + width], 'row', row_up)  11.3 us
    ppermute x3, waiting for transfers between devices, on_device(): lax.ppermute(covariance[:edge, start:start + width], 'row', row_down)  10 us
    ppermute x3, starting transfers between devices, on_device(): lax.ppermute(covariance[:edge, start:start + width], 'row', row_down)  8.11 us
    slice x2, local copies, waits for them, and re-layouts, on_device(): covariance[:edge, start:start + width]  7.26 us
    broadcast_in_dim x1, local copies, waits for them, and re-layouts, on_device(): row_coef = jnp.broadcast_to(row_coef[:, :, None], row_coef.shape + (128,))  6.85 us
  transfers between devices with their start and end apart: 8, of which 3 were waited for; matrix products, arithmetic and copies ran while one was open for 21% of the time, Pallas kernels for 20%

profile of v3, /device:TPU:2, one launch (start us, length us, event | category | flops | bytes accessed | tf_op | source)
XLA Modules:
  0.0 178.0 jit_solution(1569525286487273658)
XLA Ops:
  0.0 4.5 %fusion.42 = (f32[512,512]{1,0:T(8,128)}, f32[512,512]{1,0:T(8,128)}, f32[512,512]{1,0:T(8,128)}, f32[512,512]{1,0:T(8,128)}) fusion(f32[1024,2048]{1,0:T(8,128)} %refs_1_.5), kind=kLoop, calls=%fused_computation.121 | loop fusion | bytes 8388608 | tf_op jit(solution)/shard_map/slice | solution.py:273
  4.5 2.0 %collective-permute-start.4 = (f32[512,512]{1,0:T(8,128)}, f32[512,512]{1,0:T(8,128)S(1)}, u32[]{:S(2)}, u32[]{:S(2)}) collective-permute-start(f32[512,512]{1,0:T(8,128)} %get-tuple-element.13), channel_id=1, source_target_pairs={{4,0},{8,4},{12,8},{16,12},{20,16},{24,20},{28,24},{5,1},{9,5},{13... | collective-permute-start | bytes 3145736 | tf_op jit(solution)/shard_map/ppermute | solution.py:273
  6.6 2.4 %collective-permute-start.3 = (f32[512,512]{1,0:T(8,128)}, f32[512,512]{1,0:T(8,128)}, u32[]{:S(2)}, u32[]{:S(2)}) collective-permute-start(f32[512,512]{1,0:T(8,128)} %get-tuple-element.14), channel_id=1, source_target_pairs={{0,4},{4,8},{8,12},{12,16},{16,20},{20,24},{24,28},{1,5},{5,9},{9,... | collective-permute-start | bytes 3145736 | tf_op jit(solution)/shard_map/ppermute | solution.py:272
  9.0 3.2 %collective-permute-start.1 = (f32[512,512]{1,0:T(8,128)}, f32[512,512]{1,0:T(8,128)S(1)}, u32[]{:S(2)}, u32[]{:S(2)}) collective-permute-start(f32[512,512]{1,0:T(8,128)} %get-tuple-element.15), channel_id=1, source_target_pairs={{4,0},{8,4},{12,8},{16,12},{20,16},{24,20},{28,24},{5,1},{9,5},{13... | collective-permute-start | bytes 3145736 | tf_op jit(solution)/shard_map/ppermute | solution.py:273
  12.2 2.8 %collective-permute-start = (f32[512,512]{1,0:T(8,128)}, f32[512,512]{1,0:T(8,128)S(1)}, u32[]{:S(2)}, u32[]{:S(2)}) collective-permute-start(f32[512,512]{1,0:T(8,128)} %get-tuple-element.16), channel_id=1, source_target_pairs={{0,4},{4,8},{8,12},{12,16},{16,20},{20,24},{24,28},{1,5},{5,9},{9,... | collective-permute-start | bytes 3145736 | tf_op jit(solution)/shard_map/ppermute | solution.py:272
  15.0 2.7 %fusion.41 = (f32[512,1024]{1,0:T(8,128)}, f32[512,1024]{1,0:T(8,128)}) fusion(f32[1024,2048]{1,0:T(8,128)S(1)} %copy-done.5), kind=kLoop, calls=%fused_computation.120 | loop fusion | bytes 8388608 | tf_op jit(solution)/shard_map/slice | solution.py:273
  17.7 2.9 %collective-permute-start.6 = (f32[512,1024]{1,0:T(8,128)}, f32[512,1024]{1,0:T(8,128)}, u32[]{:S(2)}, u32[]{:S(2)}) collective-permute-start(f32[512,1024]{1,0:T(8,128)} %get-tuple-element.11), channel_id=1, source_target_pairs={{4,0},{8,4},{12,8},{16,12},{20,16},{24,20},{28,24},{5,1},{9,5},{13... | collective-permute-start | bytes 6291464 | tf_op jit(solution)/shard_map/ppermute | solution.py:273
  25.5 0.7 slice_bitcast_fusion.6
  28.8 1.5 pad_slice_fusion.1
  30.4 1.5 fusion.30
  31.9 1.5 pad_dynamic-slice_fusion.1
  33.4 0.9 copy.33
  35.0 1.5 pad_slice_fusion
  39.2 10.0 %collective-permute-done.1.refs_2_ = f32[512,512]{1,0:T(8,128)S(1)} collective-permute-done((f32[512,512]{1,0:T(8,128)}, f32[512,512]{1,0:T(8,128)S(1)}, u32[]{:S(2)}, u32[]{:S(2)}) %collective-permute-start.1) | collective-permute-done | bytes 1048608 | tf_op jit(solution)/shard_map/ppermute | solution.py:273
  49.2 1.0 copy-done.1
  50.2 6.1 %collective-permute-start.5 = (f32[512,1024]{1,0:T(8,128)}, f32[512,1024]{1,0:T(8,128)}, u32[]{:S(2)}, u32[]{:S(2)}) collective-permute-start(f32[512,1024]{1,0:T(8,128)} %get-tuple-element.12), channel_id=1, source_target_pairs={{0,4},{4,8},{8,12},{12,16},{16,20},{20,24},{24,28},{1,5},{5,9},{9,... | collective-permute-start | bytes 6291464 | tf_op jit(solution)/shard_map/ppermute | solution.py:272
  56.3 1.0 copy-done.3
  57.3 6.8 %broadcast_in_dim.20.refs_3_ = f32[10,2048,128]{2,1,0:T(8,128)} broadcast(f32[10,2048]{1,0:T(8,128)} %bitcast.203), dimensions={0,1} | broadcast | bytes 10567680 | tf_op jit(solution)/shard_map/broadcast_in_dim | solution.py:283
  64.2 9.6 %row_sections.3.refs_4_ = f32[1024,512]{1,0:T(8,128)S(1)} custom-call(f32[512,512]{1,0:T(8,128)S(1)} %copy-done.4, f32[1024,2048]{1,0:T(8,128)} %refs_1_.5, f32[512,512]{1,0:T(8,128)S(1)} %copy-done.2, f32[10,2048,128]{2,1,0:T(8,128)} %broadcast_in_dim.20.refs_3_), custom_call_target="tpu_custom_call" | custom-call | flops 31457280 | bytes 6291456 | tf_op jit(solution)/shard_map/row_sections/pallas_call | solution.py:143
  73.8 4.8 %collective-permute-start.2 = (f32[1024,512]{1,0:T(8,128)S(1)}, f32[1024,512]{1,0:T(8,128)}, u32[]{:S(2)}, u32[]{:S(2)}) collective-permute-start(f32[1024,512]{1,0:T(8,128)S(1)} %row_sections.3.refs_4_), channel_id=1, source_target_pairs={{0,1},{1,2},{2,3},{4,5},{5,6},{6,7},{8,9},{9,10},{10,11},{12,13},{... | collective-permute-start | bytes 6291464 | tf_op jit(solution)/shard_map/ppermute | solution.py:297
  78.6 10.6 %row_sections.4.refs_2_ = f32[1024,512]{1,0:T(8,128)} custom-call(f32[512,512]{1,0:T(8,128)} %collective-permute-done.3.refs_0_, f32[1024,2048]{1,0:T(8,128)} %refs_1_.5, f32[512,512]{1,0:T(8,128)S(1)} %collective-permute-done.4.refs_2_, f32[10,2048,128]{2,1,0:T(8,128)} %broadcast_in_dim.20.refs_3_), custom_call_target="tpu_custom_call" | custom-call | flops 31457280 | bytes 6291456 | tf_op jit(solution)/shard_map/row_sections/pallas_call | solution.py:143
  89.2 1.3 collective-permute-start.7
  90.5 0.9 pad_dynamic-slice_fusion
  91.6 1.6 copy.35
  93.4 2.9 %pad.65.refs_6_ = f32[3072,16]{1,0:T(8,128)} pad(f32[3072,10]{1,0:T(8,128)} %bitcast.196, f32[]{:T(128)} %constant.36.clone.1), padding=0_0x0_6 | pad | bytes 319492 | tf_op jit(solution)/shard_map/jit(_pad)/pad | solution.py:280
  96.6 0.9 fusion.35
  97.8 0.9 pad_multiply_fusion
  98.9 0.7 stack.80
  100.9 16.1 %row_sections.5.refs_3_ = f32[1024,1024]{1,0:T(8,128)} custom-call(f32[512,1024]{1,0:T(8,128)} %collective-permute-done.5.refs_0_, f32[1024,2048]{1,0:T(8,128)} %refs_1_.5, f32[512,1024]{1,0:T(8,128)} %collective-permute-done.6.refs_2_, f32[10,2048,128]{2,1,0:T(8,128)} %broadcast_in_dim.20.refs_3_), custom_call_target="tpu_custom_call" | custom-call | flops 62914560 | bytes 12582912 | tf_op jit(solution)/shard_map/row_sections/pallas_call | solution.py:143
  117.0 5.7 %collective-permute-done.2.refs_1_ = f32[1024,512]{1,0:T(8,128)} collective-permute-done((f32[1024,512]{1,0:T(8,128)S(1)}, f32[1024,512]{1,0:T(8,128)}, u32[]{:S(2)}, u32[]{:S(2)}) %collective-permute-start.2) | collective-permute-done | bytes 2097184 | tf_op jit(solution)/shard_map/ppermute | solution.py:297
  122.7 16.3 %collective-permute-done.7.refs_5_ = f32[1024,512]{1,0:T(8,128)} collective-permute-done((f32[1024,512]{1,0:T(8,128)}, f32[1024,512]{1,0:T(8,128)}, u32[]{:S(2)}, u32[]{:S(2)}) %collective-permute-start.7) | collective-permute-done | bytes 2097184 | tf_op jit(solution)/shard_map/ppermute | solution.py:295
  139.0 38.9 %col_sections.1 = f32[1024,2048]{1,0:T(8,128)} custom-call(s32[2]{0:T(128)} %pad_add_fusion.refs_0_, f32[1024,512]{1,0:T(8,128)} %collective-permute-done.2.refs_1_, f32[1024,512]{1,0:T(8,128)} %row_sections.4.refs_2_, f32[1024,1024]{1,0:T(8,128)} %row_sections.5.refs_3_, f32[1024,512]{1,0:T(8,128)} %copy-done, f32[1024,512]{1,0:T(8,128)} %collective-permute-done.7.refs_5_, ...), custom_call_target="tpu_custom_call" | custom-call | flops 125829120 | bytes 25165824 | tf_op jit(solution)/shard_map/col_sections/pallas_call | solution.py:232
  (122 shorter events, 12.7 us)
Async XLA Ops:
  0.0 15.0 %copy-start.5 = (f32[1024,2048]{1,0:T(8,128)S(1)}, f32[1024,2048]{1,0:T(8,128)}, u32[]{:S(2)}) copy-start(f32[1024,2048]{1,0:T(8,128)} %refs_1_.5) | copy-start | bytes 25165828
  4.5 74.1 %collective-permute-start.4 = (f32[512,512]{1,0:T(8,128)}, f32[512,512]{1,0:T(8,128)S(1)}, u32[]{:S(2)}, u32[]{:S(2)}) collective-permute-start(f32[512,512]{1,0:T(8,128)} %get-tuple-element.13), channel_id=1, source_target_pairs={{4,0},{8,4},{12,8},{16,12},{20,16},{24,20},{28,24},{5,1},{9,5},{13... | collective-permute-start | bytes 3145736 | tf_op jit(solution)/shard_map/ppermute | solution.py:273
  6.6 72.0 %collective-permute-start.3 = (f32[512,512]{1,0:T(8,128)}, f32[512,512]{1,0:T(8,128)}, u32[]{:S(2)}, u32[]{:S(2)}) collective-permute-start(f32[512,512]{1,0:T(8,128)} %get-tuple-element.14), channel_id=1, source_target_pairs={{0,4},{4,8},{8,12},{12,16},{16,20},{20,24},{24,28},{1,5},{5,9},{9,... | collective-permute-start | bytes 3145736 | tf_op jit(solution)/shard_map/ppermute | solution.py:272
  9.0 40.2 %collective-permute-start.1 = (f32[512,512]{1,0:T(8,128)}, f32[512,512]{1,0:T(8,128)S(1)}, u32[]{:S(2)}, u32[]{:S(2)}) collective-permute-start(f32[512,512]{1,0:T(8,128)} %get-tuple-element.15), channel_id=1, source_target_pairs={{4,0},{8,4},{12,8},{16,12},{20,16},{24,20},{28,24},{5,1},{9,5},{13... | collective-permute-start | bytes 3145736 | tf_op jit(solution)/shard_map/ppermute | solution.py:273
  12.2 8.5 %copy-start.6 = (f32[8192]{0:T(1024)S(1)}, f32[8192]{0:T(1024)}, u32[]{:S(2)}) copy-start(f32[8192]{0:T(1024)} %param.5) | copy-start | bytes 98308
  12.2 10.5 %copy-start.7 = (f32[2,64,128]{2,1,0:T(8,128)S(1)}, f32[2,64,128]{2,1,0:T(8,128)}, u32[]{:S(2)}) copy-start(f32[2,64,128]{2,1,0:T(8,128)} %param.6) | copy-start | bytes 196612
  12.2 10.6 %copy-start.8 = (f32[2,64,128]{2,1,0:T(8,128)S(1)}, f32[2,64,128]{2,1,0:T(8,128)}, u32[]{:S(2)}) copy-start(f32[2,64,128]{2,1,0:T(8,128)} %param.7) | copy-start | bytes 196612
  12.2 44.1 %collective-permute-start = (f32[512,512]{1,0:T(8,128)}, f32[512,512]{1,0:T(8,128)S(1)}, u32[]{:S(2)}, u32[]{:S(2)}) collective-permute-start(f32[512,512]{1,0:T(8,128)} %get-tuple-element.16), channel_id=1, source_target_pairs={{0,4},{4,8},{8,12},{12,16},{16,20},{20,24},{24,28},{1,5},{5,9},{9,... | collective-permute-start | bytes 3145736 | tf_op jit(solution)/shard_map/ppermute | solution.py:272
  17.7 83.1 %collective-permute-start.6 = (f32[512,1024]{1,0:T(8,128)}, f32[512,1024]{1,0:T(8,128)}, u32[]{:S(2)}, u32[]{:S(2)}) collective-permute-start(f32[512,1024]{1,0:T(8,128)} %get-tuple-element.11), channel_id=1, source_target_pairs={{4,0},{8,4},{12,8},{16,12},{20,16},{24,20},{28,24},{5,1},{9,5},{13... | collective-permute-start | bytes 6291464 | tf_op jit(solution)/shard_map/ppermute | solution.py:273
  22.8 4.7 %copy-start.11 = (f32[2,64,128]{2,1,0:T(8,128)}, f32[2,64,128]{2,1,0:T(8,128)S(1)}, u32[]{:S(2)}) copy-start(f32[2,64,128]{2,1,0:T(8,128)S(1)} %pad_maximum_fusion) | copy-start | bytes 196612
  50.2 50.7 %collective-permute-start.5 = (f32[512,1024]{1,0:T(8,128)}, f32[512,1024]{1,0:T(8,128)}, u32[]{:S(2)}, u32[]{:S(2)}) collective-permute-start(f32[512,1024]{1,0:T(8,128)} %get-tuple-element.12), channel_id=1, source_target_pairs={{0,4},{4,8},{8,12},{12,16},{16,20},{20,24},{24,28},{1,5},{5,9},{9,... | collective-permute-start | bytes 6291464 | tf_op jit(solution)/shard_map/ppermute | solution.py:272
  57.3 6.9 %copy-start.2 = (f32[512,512]{1,0:T(8,128)S(1)}, f32[512,512]{1,0:T(8,128)}, u32[]{:S(2)}) copy-start(f32[512,512]{1,0:T(8,128)} %copy-done.1) | copy-start | bytes 3145732
  57.3 6.9 %copy-start.4 = (f32[512,512]{1,0:T(8,128)S(1)}, f32[512,512]{1,0:T(8,128)}, u32[]{:S(2)}) copy-start(f32[512,512]{1,0:T(8,128)} %copy-done.3) | copy-start | bytes 3145732
  73.8 15.5 %copy-start = (f32[1024,512]{1,0:T(8,128)}, f32[1024,512]{1,0:T(8,128)S(1)}, u32[]{:S(2)}) copy-start(f32[1024,512]{1,0:T(8,128)S(1)} %row_sections.3.refs_4_) | copy-start | bytes 6291460
  73.8 48.9 %collective-permute-start.2 = (f32[1024,512]{1,0:T(8,128)S(1)}, f32[1024,512]{1,0:T(8,128)}, u32[]{:S(2)}, u32[]{:S(2)}) collective-permute-start(f32[1024,512]{1,0:T(8,128)S(1)} %row_sections.3.refs_4_), channel_id=1, source_target_pairs={{0,1},{1,2},{2,3},{4,5},{5,6},{6,7},{8,9},{9,10},{10,11},{12,13},{... | collective-permute-start | bytes 6291464 | tf_op jit(solution)/shard_map/ppermute | solution.py:297
  89.2 49.8 %collective-permute-start.7 = (f32[1024,512]{1,0:T(8,128)}, f32[1024,512]{1,0:T(8,128)}, u32[]{:S(2)}, u32[]{:S(2)}) collective-permute-start(f32[1024,512]{1,0:T(8,128)} %row_sections.4.refs_2_), channel_id=1, source_target_pairs={{1,0},{2,1},{3,2},{5,4},{6,5},{7,6},{9,8},{10,9},{11,10},{13,12},{... | collective-permute-start | bytes 6291464 | tf_op jit(solution)/shard_map/ppermute | solution.py:295
  93.2 3.4 %copy-start.25 = (f32[64,127]{1,0:T(8,128)S(1)}, f32[64,127]{1,0:T(8,128)}, u32[]{:S(2)}) copy-start(f32[64,127]{1,0:T(8,128)} %get-tuple-element.91) | copy-start | bytes 97540
  93.2 3.4 %copy-start.28 = (f32[64,1]{1,0:T(8,128)S(1)}, f32[64,1]{1,0:T(8,128)}, u32[]{:S(2)}) copy-start(f32[64,1]{1,0:T(8,128)} %get-tuple-element.50) | copy-start | bytes 772
  93.2 3.4 %copy-start.29 = (f32[64,1]{1,0:T(8,128)S(1)}, f32[64,1]{1,0:T(8,128)}, u32[]{:S(2)}) copy-start(f32[64,1]{1,0:T(8,128)} %get-tuple-element.89) | copy-start | bytes 772
  93.2 3.4 %copy-start.30 = (f32[62,128]{1,0:T(8,128)S(1)}, f32[62,128]{1,0:T(8,128)}, u32[]{:S(2)}) copy-start(f32[62,128]{1,0:T(8,128)} %get-tuple-element.44) | copy-start | bytes 95236
  93.3 3.4 %copy-start.39 = (f32[64,1]{1,0:T(8,128)S(1)}, f32[64,1]{1,0:T(8,128)}, u32[]{:S(2)}) copy-start(f32[64,1]{1,0:T(8,128)} %get-tuple-element.54) | copy-start | bytes 772
  93.3 4.2 %copy-start.10 = (f32[2,64,128]{2,1,0:T(8,128)S(1)}, f32[2,64,128]{2,1,0:T(8,128)}, u32[]{:S(2)}) copy-start(f32[2,64,128]{2,1,0:T(8,128)} %copy-done.9) | copy-start | bytes 196612
  93.3 4.2 %copy-start.16 = (f32[64,1,2]{2,0,1:T(8,128)S(1)}, f32[64,1,2]{2,0,1:T(8,128)}, u32[]{:S(2)}) copy-start(f32[64,1,2]{2,0,1:T(8,128)} %get-tuple-element.61) | copy-start | bytes 1540
  93.3 4.2 %copy-start.17 = (f32[64,1,126]{2,0,1:T(8,128)S(1)}, f32[64,1,126]{2,0,1:T(8,128)}, u32[]{:S(2)}) copy-start(f32[64,1,126]{2,0,1:T(8,128)} %get-tuple-element.59) | copy-start | bytes 96772
  93.3 4.2 %copy-start.35 = (f32[64,1,127]{2,0,1:T(8,128)S(1)}, f32[64,1,127]{2,0,1:T(8,128)}, u32[]{:S(2)}) copy-start(f32[64,1,127]{2,0,1:T(8,128)} %get-tuple-element.63) | copy-start | bytes 97540
  93.3 4.2 %copy-start.36 = (f32[64,1,1]{2,0,1:T(8,128)S(1)}, f32[64,1,1]{2,0,1:T(8,128)}, u32[]{:S(2)}) copy-start(f32[64,1,1]{2,0,1:T(8,128)} %get-tuple-element.65) | copy-start | bytes 772
  93.3 4.4 %copy-start.13 = (f32[63,128]{1,0:T(8,128)S(1)}, f32[63,128]{1,0:T(8,128)}, u32[]{:S(2)}) copy-start(f32[63,128]{1,0:T(8,128)} %get-tuple-element.58) | copy-start | bytes 96772
  93.3 4.4 %copy-start.20 = (f32[64,127]{1,0:T(8,128)S(1)}, f32[64,127]{1,0:T(8,128)}, u32[]{:S(2)}) copy-start(f32[64,127]{1,0:T(8,128)} %get-tuple-element.92) | copy-start | bytes 97540
  93.3 4.4 %copy-start.22 = (f32[64,1]{1,0:T(8,128)S(1)}, f32[64,1]{1,0:T(8,128)}, u32[]{:S(2)}) copy-start(f32[64,1]{1,0:T(8,128)} %get-tuple-element.90) | copy-start | bytes 772
  93.4 4.4 %copy-start.23 = (f32[62,128]{1,0:T(8,128)S(1)}, f32[62,128]{1,0:T(8,128)}, u32[]{:S(2)}) copy-start(f32[62,128]{1,0:T(8,128)} %get-tuple-element.43) | copy-start | bytes 95236
  93.4 4.4 %copy-start.26 = (f32[63,128]{1,0:T(8,128)S(1)}, f32[63,128]{1,0:T(8,128)}, u32[]{:S(2)}) copy-start(f32[63,128]{1,0:T(8,128)} %get-tuple-element.55) | copy-start | bytes 96772
  93.4 4.4 %copy-start.27 = (f32[63,128]{1,0:T(8,128)S(1)}, f32[63,128]{1,0:T(8,128)}, u32[]{:S(2)}) copy-start(f32[63,128]{1,0:T(8,128)} %get-tuple-element.56) | copy-start | bytes 96772
  (17 other events, 43.1 us)
